TPU v7x, 32 devices: a whole 2x2x4 slice. The times are simulated.
32 devices in a mesh: case: 4 (over z), gx: 2 (over y), gy: 4 (over x, core).
Axes of the slice: x: 2, y: 2, z: 4, core: 2. Of those that a mesh axis runs over, the one named last changes fastest.
Arguments:
- velocity: bfloat16 [4, 3, 32, 64, 128], P('case', None, 'gx', 'gy'), may hold values from -4 to 3
- target: bfloat16 [4, 3, 32, 64, 128], P('case', None, 'gx', 'gy'), may hold values from -3 to 3
- weight_in: bfloat16 [256, 12], replicated, may hold values from -1.75 to 1.75
- bias_in: float32 [256], replicated, may hold values from -3 to 3
- weight_mid: bfloat16 [256, 256], replicated, may hold values from -0.375 to 0.375
- bias_mid: float32 [256], replicated, may hold values from -3 to 3
- weight_out: bfloat16 [3, 256], replicated, may hold values from -0.375 to 0.375
- bias_out: float32 [3], replicated, may hold values from -3 to 3
- thrust_coef: float32 [100], replicated, may hold values from 0.5 to 1
- tile_cells: int32 [64, 128], P(('gx', 'gy')), may hold values from 0 to 32767
- tile_turbine: int32 [64], P(('gx', 'gy')), may hold values from -1 to 99, as said below
- tile_weight: float32 [64, 128], P(('gx', 'gy')), may hold values from 0.25 to 2
Outputs:
- velocity_new: bfloat16 [4, 3, 32, 64, 128], P('case', None, 'gx', 'gy')
- loss: float32 [], replicated
- step_weight_in: float32 [256, 12], replicated
- step_bias_in: float32 [256], replicated
- step_weight_mid: float32 [256, 256], replicated
- step_bias_mid: float32 [256], replicated
- step_weight_out: float32 [3, 256], replicated
- step_bias_out: float32 [3], replicated
- force_grad: bfloat16 [4, 3, 32, 64, 128], P('case', None, 'gx', 'gy')
Inputs may be any that keep to these rules, and one draw needn't show every extreme that they name: `tile_turbine`: in each device's block of 8 tile rows the used rows come first and the rest hold -1; in every draw some device has all 8 rows used.
All inputs are finite; a program needn't handle non-finite values.
Results may differ from a plain program's by a relative error of at most 0.0006.
The roundings to bfloat16 on the way count: a program that leaves them out, or rounds other values in their place, can miss the bound.
Values may be sent and summed in bfloat16 or wider, within the bound.
No kernel may reach another device: no remote copies, remote signals or barrier semaphores. Data moves between devices by JAX's collectives and lax.ppermute only.
A program may use at most 128 MiB of HBM per device.

v0:
```python
import functools

import jax
import jax.numpy as jnp
import numpy as np
from jax import lax
from jax.experimental import pallas as pl
from jax.experimental.pallas import tpu as pltpu
from jax.sharding import PartitionSpec as P


ITERS = 20
INFLOW = 1.0
STEP_DT = 0.4
VISCOSITY = 0.1
EPSILON_RMS = 1e-06

F32 = jnp.float32
BF16 = jnp.bfloat16
VMEM = pltpu.VMEM
MIB = 1024 * 1024
LIMIT = 58 * MIB
ROOM = 60 * 1024 * 1024


def parity_of(dim):
    return lax.axis_index(("gx", "gy")[dim]) & 1


def vspec():
    return pl.BlockSpec(memory_space=pltpu.VMEM)


def sspec():
    return pl.BlockSpec(memory_space=pltpu.SMEM)


def dot(a, b):
    return lax.dot_general(a, b, (((1,), (0,)), ((), ())), preferred_element_type=F32)


def dot_nt(a, b):
    return lax.dot_general(a, b, (((1,), (1,)), ((), ())), preferred_element_type=F32)


def dot_full(a, b):
    return lax.dot_general(
        a, b, (((1,), (0,)), ((), ())), precision=lax.Precision.HIGHEST, preferred_element_type=F32
    )


def depth_basis(depth):
    mode = np.arange(1, depth + 1, dtype=np.float64)
    basis = np.sqrt(2.0 / (depth + 1)) * np.sin(np.pi * np.outer(mode, mode) / (depth + 1))
    slope = 0.5 * (np.eye(depth, k=-1) - np.eye(depth, k=1))
    matrices = np.stack([basis, basis @ slope, basis @ slope @ slope @ basis])
    return matrices.astype(np.float32), (2.0 * np.cos(np.pi * mode / (depth + 1))).astype(np.float32)[None]


def lane_shifts(values, step=1):
    depth = values.shape[-1]
    axis = values.ndim - 1
    lane = lax.broadcasted_iota(jnp.int32, values.shape, axis)
    up = jnp.where(lane < depth - step, pltpu.roll(values, depth - step, axis), 0.0)
    down = jnp.where(lane >= step, pltpu.roll(values, step, axis), 0.0)
    return up, down


def start_kernel(cells_ref, turbine_ref, weight_ref, v_ref, t_ref, *outs):
    n_x_sends = (len(outs) - 1) // 2 if False else None
    del n_x_sends
    face_refs, disk_ref = outs[:-1], outs[-1]
    span_x, span_y, depth = v_ref.shape[1:]
    for ref, (dim, high_parity) in zip(face_refs, start_kernel.plan):
        take_high = parity_of(dim) == high_parity
        for part, source in enumerate((v_ref, t_ref)):
            for c in range(3):
                if dim == 0:
                    high, low = source[c, span_x - 1], source[c, 0]
                    ref[3 * part + c] = jnp.where(take_high, high.astype(F32), low.astype(F32)).astype(BF16)
                else:
                    for x in range(span_x):
                        plane = source[c, x].astype(F32)
                        row = jnp.where(take_high, plane[span_y - 1 : span_y], plane[0:1])
                        ref[3 * part + c, x : x + 1, :] = row.astype(BF16)
    rows = span_x * span_y
    tiles, width = cells_ref.shape
    stream = v_ref[0].astype(F32).reshape(rows, depth).T.astype(BF16)
    pick = []
    for r in range(tiles):
        cell_row = cells_ref[r : r + 1, :] // depth
        spot = lax.broadcasted_iota(jnp.int32, (rows, width), 0)
        pick.append((spot == cell_row).astype(F32).astype(BF16))
    found = dot(stream, jnp.concatenate(pick, 1))
    turbines = disk_ref.shape[1]
    lane = lax.broadcasted_iota(jnp.int32, (1, turbines), 1)
    total = jnp.zeros((1, turbines), F32)
    area = jnp.zeros((1, turbines), F32)
    spot = lax.broadcasted_iota(jnp.int32, (depth, width), 0)
    for r in range(tiles):
        cell_lane = cells_ref[r : r + 1, :] % depth
        values = jnp.sum(jnp.where(spot == cell_lane, found[:, r * width : (r + 1) * width], 0.0), 0, keepdims=True)
        weight = weight_ref[r : r + 1, :]
        weighted = jnp.sum(weight * (values + INFLOW), 1, keepdims=True)
        summed = jnp.sum(weight, 1, keepdims=True)
        mine = lane == turbine_ref[r]
        total = total + jnp.where(mine, weighted, 0.0)
        area = area + jnp.where(mine, summed, 0.0)
    disk_ref[...] = jnp.zeros_like(disk_ref)
    disk_ref[0:1, :] = total
    disk_ref[1:2, :] = area


def fill_padded(pad, source, first, faces, plan):
    span_x, span_y = source.shape[1], source.shape[2]
    depth = source.shape[3]
    zero_plane = jnp.zeros((span_y, depth), F32)
    zero_rows = jnp.zeros((span_x, depth), F32)
    for c in range(3):
        for x in range(span_x):
            pad[c, 1 + x, 8 : 8 + span_y, :] = source[c, x].astype(F32)
        low = {0: zero_plane, 1: zero_rows}
        high = {0: zero_plane, 1: zero_rows}
        for ref, (dim, high_parity) in zip(faces, plan):
            got = ref[first + c].astype(F32)
            is_high = parity_of(dim) == high_parity
            high[dim] = jnp.where(is_high, got, high[dim])
            low[dim] = jnp.where(is_high, low[dim], got)
        pad[c, 0, 8 : 8 + span_y, :] = low[0]
        pad[c, 1 + span_x, 8 : 8 + span_y, :] = high[0]
        for x in range(span_x):
            pad[c, 1 + x, 7:8, :] = low[1][x : x + 1]
            pad[c, 1 + x, 8 + span_y : 9 + span_y, :] = high[1][x : x + 1]


def forward_kernel(plan, n_faces, *refs):
    faces = refs[:n_faces]
    (
        v_ref, w_in_t, b_in, w_mid, b_mid, w_out, b_out,
        one_ref, two_ref, feat_ref, closure_ref,
        pad, stage, stage_out, w_in, b_column, held,
    ) = refs[n_faces:]
    span_y, depth = v_ref.shape[2], v_ref.shape[3]
    planes = closure_ref.shape[1]
    lines = planes * span_y
    i = pl.program_id(0)

    def prepare(step):
        for k in range(planes):
            x = step * planes + k
            own = slice(8, 8 + span_y)

            def put(channel, value):
                stage[pl.ds(16 * span_y * k + channel, span_y, stride=16), :] = value

            for c in range(3):
                centre = pad[c, x + 1, own, :]
                put(c, 0.5 * (pad[c, x + 2, own, :] - pad[c, x, own, :]))
                put(3 + c, 0.5 * (pad[c, x + 1, 9 : 9 + span_y, :] - pad[c, x + 1, 7 : 7 + span_y, :]))
                up, down = lane_shifts(centre)
                put(6 + c, 0.5 * (up - down))
                put(9 + c, centre)
        held[...] = jnp.concatenate([stage[16 * y : 16 * y + 16, :].astype(BF16) for y in range(lines)], 1)

    def begin(k, carry):
        fill_padded(pad, v_ref, 0, faces, plan)
        channel = lax.broadcasted_iota(jnp.int32, stage.shape, 0) % 16
        stage[...] = jnp.where((channel >= 12) & (channel < 15), 1.0, 0.0)
        bias = b_in[...]
        high = bias.astype(BF16).astype(F32)
        rest = bias - high
        middle = rest.astype(BF16).astype(F32)
        rows = jnp.concatenate([w_in_t[...].astype(F32), high, middle, rest - middle, jnp.zeros_like(bias)], 0)
        w_in[...] = rows.T.astype(BF16)
        b_column[...] = jnp.broadcast_to(b_mid[...], (8, bias.shape[1])).T
        prepare(0)
        return carry

    lax.fori_loop(0, jnp.where(i == 0, 1, 0), begin, 0)

    features = held[...]
    feat_ref[...] = features
    prepare(jnp.minimum(i + 1, pl.num_programs(0) - 1))
    hidden_one = jnp.tanh(dot(w_in[...], features)).astype(BF16)
    one_ref[...] = hidden_one
    hidden_two = jnp.tanh(dot(w_mid[...], hidden_one) + b_column[:, 0:1]).astype(BF16)
    two_ref[...] = hidden_two
    out = dot(w_out[...], hidden_two)
    for y in range(lines):
        stage_out[8 * y : 8 * y + 3, :] = out[:, y * depth : (y + 1) * depth]
    for k in range(planes):
        for c in range(3):
            closure_ref[c, k] = stage_out[pl.ds(8 * span_y * k + c, span_y, stride=8), :] + b_out[c]


def provisional_kernel(plan, n_faces, n_disks, turbine_ref, *refs):
    faces = refs[:n_faces]
    disks = refs[n_faces : n_faces + n_disks]
    (cells_ref, weight_ref, coef_ref, v_ref, t_ref, closure_ref, basis_ref, prov_ref, first_out, second_out, pad, force, qpad, first_ref, second_ref) = refs[
        n_faces + n_disks :
    ]
    span_x, span_y, depth = v_ref.shape[1:]
    rows = span_x * span_y
    tiles, width = cells_ref.shape
    half = span_x // 2
    sums = disks[0][...]
    for extra in disks[1:]:
        sums = sums + extra[...]
    speed = sums[0:1, :] / jnp.maximum(sums[1:2, :], 1.0)
    thrust = -0.5 * coef_ref[...] * speed * jnp.abs(speed)
    lane = lax.broadcasted_iota(jnp.int32, thrust.shape, 1)
    spot_row = lax.broadcasted_iota(jnp.int32, (rows, width), 0)
    spot_lane = lax.broadcasted_iota(jnp.int32, (depth, width), 0)
    pick, spread = [], []
    for r in range(tiles):
        row_thrust = jnp.sum(jnp.where(lane == turbine_ref[r], thrust, 0.0), 1, keepdims=True)
        strength = weight_ref[r : r + 1, :] * row_thrust
        cell = cells_ref[r : r + 1, :]
        pick.append((spot_row == cell // depth).astype(F32).astype(BF16))
        spread.append(jnp.where(spot_lane == cell % depth, strength, 0.0))
    pick = jnp.concatenate(pick, 1)
    spread = jnp.concatenate(spread, 1)
    hi = spread.astype(BF16)
    rest = spread - hi.astype(F32)
    mid = rest.astype(BF16)
    low = (rest - mid.astype(F32)).astype(BF16)
    force[...] = dot_nt(pick, hi) + (dot_nt(pick, mid) + dot_nt(pick, low))

    fill_padded(pad, t_ref, 3, faces, plan)
    for x in range(span_x):
        up, down = lane_shifts(pad[2, x + 1, 8 : 8 + span_y, :])
        value = (
            0.5 * (pad[0, x + 2, 8 : 8 + span_y, :] - pad[0, x, 8 : 8 + span_y, :])
            + 0.5 * (pad[1, x + 1, 9 : 9 + span_y, :] - pad[1, x + 1, 7 : 7 + span_y, :])
            + 0.5 * (up - down)
        )
        where_to = first_ref if x < half else second_ref
        where_to[half + x % half] = value

    fill_padded(pad, v_ref, 0, faces, plan)
    qpad[...] = jnp.zeros_like(qpad)
    for x in range(span_x):
        centre = [pad[c, x + 1, 8 : 8 + span_y, :] for c in range(3)]
        for c in range(3):
            xp, xm = pad[c, x + 2, 8 : 8 + span_y, :], pad[c, x, 8 : 8 + span_y, :]
            yp, ym = pad[c, x + 1, 9 : 9 + span_y, :], pad[c, x + 1, 7 : 7 + span_y, :]
            zp, zm = lane_shifts(centre[c])
            laplace = (xp + xm) + yp + ym + zp + zm - 6.0 * centre[c]
            advect = (
                (centre[0] + INFLOW) * (0.5 * (xp - xm)) + centre[1] * (0.5 * (yp - ym)) + centre[2] * (0.5 * (zp - zm))
            )
            tendency = VISCOSITY * laplace - advect + closure_ref[c, x]
            if c == 0:
                tendency = tendency + force[x * span_y : (x + 1) * span_y, :]
            value = (centre[c] + STEP_DT * tendency).astype(BF16)
            prov_ref[c, x] = value
            qpad[c, 1 + x, 8 : 8 + span_y, :] = value.astype(F32)
    for x in range(span_x):
        up, down = lane_shifts(qpad[2, x + 1, 8 : 8 + span_y, :])
        value = (
            0.5 * (qpad[0, x + 2, 8 : 8 + span_y, :] - qpad[0, x, 8 : 8 + span_y, :])
            + 0.5 * (qpad[1, x + 1, 9 : 9 + span_y, :] - qpad[1, x + 1, 7 : 7 + span_y, :])
            + 0.5 * (up - down)
        )
        where_to = first_ref if x < half else second_ref
        where_to[x % half] = value
        second_ref[2 * half, x : x + 1, :] = 0.5 * qpad[1, 1 + x, 8:9, :]
        second_ref[2 * half + 1, x : x + 1, :] = -0.5 * qpad[1, 1 + x, 7 + span_y : 8 + span_y, :]
    first_ref[2 * half] = 0.5 * qpad[0, 1, 8 : 8 + span_y, :]
    first_ref[2 * half + 1] = -0.5 * qpad[0, span_x, 8 : 8 + span_y, :]
    for scratch, out in ((first_ref, first_out), (second_ref, second_out)):
        out[...] = dot_full(scratch[...].reshape(-1, depth), basis_ref[0]).reshape(out.shape)


def solve_kernel(offsets, n_x, n_y, *refs):
    n = len(offsets)
    firsts, seconds = refs[:n], refs[n : 2 * n]
    q_ref, t_ref, basis_ref, modes_ref, new_ref, grad_ref, cost_ref, div, div_t, source, pa, pb, seed, moved, twice = refs[2 * n :]
    span_x, span_y, depth = q_ref.shape[1:]
    total_x, total_y = source.shape[0], source.shape[1]
    half = span_x // 2
    rows = slice(8, 8 + total_y)
    ix, iy = lax.axis_index("gx"), lax.axis_index("gy")

    for buffer in (pa, pb):
        for edge in (buffer.at[0:2], buffer.at[total_x + 2 : total_x + 4], buffer.at[:, 0:8], buffer.at[:, 8 + total_y :]):
            edge[...] = jnp.zeros(edge.shape, F32)
    spots = []
    for mx, my in offsets:
        spots.append((partner(ix, mx, total_x // span_x) * span_x, pl.multiple_of(partner(iy, my, total_y // span_y) * span_y, span_y)))
    for k, (x0, y0) in enumerate(spots):
        for ref, base in ((firsts[k], 0), (seconds[k], half)):
            for x in range(half):
                div[x0 + base + x + 1, pl.ds(pl.multiple_of(y0 + 8, 8), span_y), :] = ref[x]
                div_t[x0 + base + x, pl.ds(y0, span_y), :] = ref[half + x]
    for k, (x0, y0) in enumerate(spots):
        own = pl.ds(pl.multiple_of(y0 + 8, 8), span_y)
        div[x0, own, :] = div[x0, own, :] + firsts[k][2 * half]
        div[x0 + span_x + 1, own, :] = div[x0 + span_x + 1, own, :] + firsts[k][2 * half + 1]
        for x in range(span_x):
            below = pl.ds(y0 + 7, 1)
            above = pl.ds(y0 + 8 + span_y, 1)
            div[x0 + x + 1, below, :] = div[x0 + x + 1, below, :] + seconds[k][2 * half, x : x + 1, :]
            div[x0 + x + 1, above, :] = div[x0 + x + 1, above, :] + seconds[k][2 * half + 1, x : x + 1, :]

    unit = 1.0 / (6.0 * STEP_DT)

    def first_source(x, carry):
        value = div[x + 1, rows, :] * unit
        source[x] = value
        pa[x + 2, rows, :] = -value
        return carry

    lax.fori_loop(0, total_x, first_source, 0, unroll=4)

    def sweep(src, dst, x_start, x_count, y_start, y_count):
        own = pl.ds(y_start + 8, y_count)
        mode = modes_ref[...]
        group = x_count if x_count <= 32 else 32

        def planes(i, carry):
            base = x_start + i * group
            loaded = {}

            def plane(k):
                if k not in loaded:
                    loaded[k] = src[base + k, own, :]
                return loaded[k]

            for k in range(group):
                centre = plane(k + 2)
                across = plane(k + 1) + plane(k + 3)
                beside = src[base + k + 2, pl.ds(y_start + 9, y_count), :] + src[base + k + 2, pl.ds(y_start + 7, y_count), :]
                around = (across + beside) + mode * centre
                dst[base + k + 2, own, :] = around * (1.0 / 6.0) - source[base + k, pl.ds(y_start, y_count), :]
                loaded.pop(k + 1)
            return carry

        if x_count == group:
            planes(0, 0)
        else:
            lax.fori_loop(0, x_count // group, planes, 0)

    def run(stages, start=0):
        buffers, now = (pa, pb), start
        for window, count in stages:

            def two(k, carry, now=now, window=window):
                sweep(buffers[now], buffers[1 - now], *window)
                sweep(buffers[1 - now], buffers[now], *window)
                return carry

            if count // 2:
                lax.fori_loop(0, count // 2, two, 0)
            if count % 2:
                sweep(buffers[now], buffers[1 - now], *window)
                now = 1 - now
        return buffers[now]

    whole = (0, total_x, 0, total_y)

    def windows():
        stages = []
        left = ITERS - 1
        for k in range(left):
            margin = -(-(left - k) // 8) * 8
            x_count = min(total_x, span_x + margin * min(n_x - 1, 2))
            y_count = min(total_y, span_y + margin * min(n_y - 1, 2))
            key = (margin, x_count, y_count)
            if stages and (stages[-1][0][1:] == key[1:]):
                stages[-1][1] += 1
            else:
                stages.append([key, 1])
        result = []
        for (margin, x_count, y_count), count in stages:
            x_start = 0 if x_count == total_x else jnp.clip(ix * span_x - margin, 0, total_x - x_count)
            y_start = 0
            if y_count != total_y:
                y_start = pl.multiple_of(jnp.clip(iy * span_y - margin, 0, total_y - y_count), 8)
            result.append(((x_start, x_count, y_start, y_count), count))
        return result

    def correction(p):
        y0 = pl.multiple_of(iy * span_y, 8)
        own = pl.ds(pl.multiple_of(y0 + 8, 8), span_y)
        for x in range(span_x):
            at = ix * span_x + x + 2
            wide = p[at, pl.ds(y0, span_y + 16), :]
            lines = slice(x * span_y, (x + 1) * span_y)
            moved[0, lines, :] = (0.5 * STEP_DT) * (p[at + 1, own, :] - p[at - 1, own, :])
            moved[1, lines, :] = (0.5 * STEP_DT) * (wide[9 : 9 + span_y] - wide[7 : 7 + span_y])
            moved[2, lines, :] = STEP_DT * wide[8 : 8 + span_y]
        for c in range(3):
            moved[c] = dot_full(moved[c], basis_ref[0 if c < 2 else 1])

    p = run([(whole, ITERS - 1)])
    cost = jnp.zeros((span_y, depth), F32)
    correction(p)
    for x in range(span_x):
        for c in range(3):
            updated = q_ref[c, x].astype(F32) - moved[c, x * span_y : (x + 1) * span_y, :]
            new_ref[c, x] = updated.astype(BF16)
            mismatch = updated - t_ref[c, x].astype(F32)
            cost = cost + mismatch * mismatch
            seed[c, x] = 2.0 * mismatch
    cost_ref[...] = cost[0:8] + sum((cost[k : k + 8] for k in range(8, span_y, 8)), jnp.zeros((8, depth), F32))

    other = pa if p is pb else pb
    together = 8

    def vertical(i, carry):
        some = pl.ds(i * together, together)
        values = p[pl.ds(i * together + 2, together), rows, :].reshape(-1, depth)
        twice[some] = dot_full(values, basis_ref[2]).reshape(together, total_y, depth)
        return carry

    lax.fori_loop(0, total_x // together, vertical, 0)

    def second_source(x, carry):
        centre = p[x + 2, rows, :]
        to_high = jnp.where(x + 1 < total_x, 0.25, 0.0)
        to_low = jnp.where(x > 0, 0.25, 0.0)
        wide = to_high * (p[x + 4, rows, :] - centre) - to_low * (centre - p[x, rows, :])
        row = lax.broadcasted_iota(jnp.int32, centre.shape, 0)
        wide = wide + 0.25 * (
            jnp.where(row < total_y - 1, p[x + 2, 10 : 10 + total_y, :] - centre, 0.0)
            - jnp.where(row > 0, centre - p[x + 2, 6 : 6 + total_y, :], 0.0)
        )
        wide = wide + twice[x]
        value = (2.0 * unit) * (div[x + 1, rows, :] - STEP_DT * wide - div_t[x])
        source[x] = value
        other[x + 2, rows, :] = -value
        return carry

    lax.fori_loop(0, total_x, second_source, 0, unroll=4)
    p = run(windows(), start=0 if p is pb else 1)
    correction(p)
    for x in range(span_x):
        for c in range(3):
            grad_ref[c, x] = (STEP_DT * (seed[c, x] - moved[c, x * span_y : (x + 1) * span_y, :])).astype(BF16)


def backward_kernel(n_sums, grad_ref, feat_ref, one_ref, two_ref, w_out, w_mid, cost_ref, *refs):
    sum_refs = refs[:n_sums]
    stage, acc_mid, acc_in, acc_out, acc_b, w_out_t, w_mid_t, whole = refs[n_sums:]
    planes, span_y, depth = grad_ref.shape[1:]
    lines = planes * span_y
    units = one_ref.shape[0]
    i = pl.program_id(0)

    @pl.when(i == 0)
    def _():
        stage[...] = jnp.zeros_like(stage)
        acc_mid[...] = jnp.zeros_like(acc_mid)
        acc_in[...] = jnp.zeros_like(acc_in)
        acc_out[...] = jnp.zeros_like(acc_out)
        acc_b[...] = jnp.zeros_like(acc_b)
        out = jnp.concatenate([w_out[...].astype(F32), jnp.zeros((13, units), F32)], 0)
        w_out_t[...] = out.T.astype(BF16)
        w_mid_t[...] = w_mid[...].astype(F32).T.astype(BF16)

    for k in range(planes):
        for c in range(3):
            stage[pl.ds(16 * span_y * k + c, span_y, stride=16), :] = grad_ref[c, k].astype(F32)
    grad = jnp.concatenate([stage[16 * y : 16 * y + 16, :].astype(BF16) for y in range(lines)], 1)
    bias = stage[0:8, :]
    for y in range(1, lines):
        bias = bias + stage[16 * y : 16 * y + 8, :]
    acc_b[...] += bias
    hidden_one, hidden_two = one_ref[...], two_ref[...]
    two_value = hidden_two.astype(F32)
    delta_two = (dot(w_out_t[...], grad) * (1.0 - two_value * two_value)).astype(BF16)
    ones = jnp.ones((16, hidden_one.shape[1]), BF16)
    acc_mid[...] += dot_nt(jnp.concatenate([hidden_one, ones], 0), delta_two)
    one_value = hidden_one.astype(F32)
    delta_one = (dot(w_mid_t[...], delta_two) * (1.0 - one_value * one_value)).astype(BF16)
    acc_out[...] += dot_nt(grad, hidden_two)
    acc_in[...] += dot_nt(feat_ref[...], delta_one)

    @pl.when(i == pl.num_programs(0) - 1)
    def _():
        whole[...] = jnp.zeros_like(whole)
        whole[0:units, :] = acc_mid[0:units, :]
        whole[units : units + 13, :] = acc_in[0:13, :]
        whole[units + 13 : units + 14, :] = acc_mid[units : units + 1, :]
        whole[units + 14 : units + 17, :] = acc_out[0:3, :]
        lane = lax.broadcasted_iota(jnp.int32, (1, units), 1)
        row = jnp.where(lane == 3, jnp.sum(cost_ref[...]), 0.0)
        for c in range(3):
            row = row + jnp.where(lane == c, jnp.sum(acc_b[c : c + 1, :]), 0.0)
        whole[units + 17 : units + 18, :] = row
        if len(sum_refs) == 1:
            sum_refs[0][...] = whole[...]
        else:
            size = sum_refs[0].shape[0]
            mine = parity_of(1)
            sum_refs[0][...] = whole[pl.ds(pl.multiple_of(mine * size, 8), size), :]
            sum_refs[1][...] = whole[pl.ds(pl.multiple_of((1 - mine) * size, 8), size), :]


def finish_kernel(spot_of, entry_total, cell_total, *refs):
    n = len(refs) - 8
    pieces = refs[:n]
    loss_ref, in_ref, b_in_ref, mid_ref, b_mid_ref, out_ref, b_out_ref, whole = refs[n:]
    units = mid_ref.shape[0]
    feats = in_ref.shape[0]
    size = pieces[0].shape[0]
    for ref, spot in zip(pieces, spot_of()):
        whole[pl.ds(pl.multiple_of(spot * size, 8), size), :] = ref[...]
    mid = whole[0:units, :]
    small = whole[units : units + 32, :]
    row = lax.broadcasted_iota(jnp.int32, small.shape, 0)
    lane = lax.broadcasted_iota(jnp.int32, small.shape, 1)
    counted = (row < feats + 5) | ((row == feats + 5) & (lane < 3))
    squares = jnp.sum(mid * mid) + jnp.sum(jnp.where(counted, small * small, 0.0))
    scale = jnp.full((1, 1), 1.0, F32) / jnp.sqrt(jnp.full((1, 1), 1.0, F32) * squares / entry_total + EPSILON_RMS)
    small = small * scale
    mid_ref[...] = (mid * scale).T
    in_ref[...] = small[0:feats]
    b_in_ref[...] = small[feats : feats + 1]
    b_mid_ref[...] = small[feats + 1 : feats + 2]
    out_ref[...] = small[feats + 2 : feats + 5]
    b_out_ref[...] = small[feats + 5 : feats + 6, 0:3]
    loss_ref[...] = whole[units + feats + 5 : units + feats + 6, 3:4] / cell_total


def is_power(count):
    return count & (count - 1) == 0


def partner(index, step, count):
    return index ^ step if is_power(count) else (index + step) % count


def pair_list(count, offset):
    pairs = []
    for low in range(offset, count - 1, 2):
        pairs += [(low, low + 1), (low + 1, low)]
    return pairs


def face_plan(n_x, n_y):
    plan = []
    for dim, count in ((0, n_x), (1, n_y)):
        if count > 1:
            plan.append((dim, 0))
        if count > 2:
            plan.append((dim, 1))
    return tuple(plan)


def swap(values, axis, step):
    count = lax.axis_size(axis)
    return lax.ppermute(values, axis, [(i, partner(i, step, count)) for i in range(count)])


def swap_both(values, step_x, step_y):
    n_x, n_y = lax.axis_size("gx"), lax.axis_size("gy")
    pairs = [
        (i * n_y + j, partner(i, step_x, n_x) * n_y + partner(j, step_y, n_y)) for i in range(n_x) for j in range(n_y)
    ]
    return lax.ppermute(values, ("gx", "gy"), pairs)


def gather_doubling(values, order):
    held = {(0, 0): values}
    for axis, bit in order:
        for (sx, sy), block in list(held.items()):
            key = (sx ^ bit, sy) if axis == "gx" else (sx, sy ^ bit)
            held[key] = swap(block, axis, bit)
    return held


def bits_of(axis, count):
    return [(axis, 1 << k) for k in reversed(range(count.bit_length() - 1))]


def on_device(
    velocity,
    target,
    weight_in,
    bias_in,
    weight_mid,
    bias_mid,
    weight_out,
    bias_out,
    thrust_coef,
    tile_cells,
    tile_turbine,
    tile_weight,
):
    stay = lambda x: pltpu.with_memory_space_constraint(x, pltpu.HBM)
    v, t = stay(velocity[0]), stay(target[0])
    _, span_x, span_y, depth = v.shape
    units, feats = weight_in.shape
    cells = span_x * span_y * depth
    turbines = thrust_coef.shape[0]
    n_case, n_x, n_y = lax.axis_size("case"), lax.axis_size("gx"), lax.axis_size("gy")
    ix, iy = lax.axis_index("gx"), lax.axis_index("gy")
    plan = face_plan(n_x, n_y)
    shape_of = jax.ShapeDtypeStruct

    start_kernel.plan = plan
    started = pl.pallas_call(
        start_kernel,
        name="start",
        out_shape=tuple(shape_of((6, span_y if d == 0 else span_x, depth), BF16) for d, _ in plan)
        + (shape_of((8, turbines), F32),),
        in_specs=[vspec(), sspec(), vspec(), vspec(), vspec()],
        out_specs=tuple(vspec() for _ in range(len(plan) + 1)),
        compiler_params=pltpu.CompilerParams(vmem_limit_bytes=LIMIT),
    )(tile_cells, tile_turbine, tile_weight, v, t)
    disk = started[-1]
    faces = []
    for face, (dim, parity) in zip(started[:-1], plan):
        axis, count = (("gx", n_x), ("gy", n_y))[dim]
        faces.append(lax.ppermute(face, axis, pair_list(count, parity)))
    if n_y > 1 and is_power(n_y) and is_power(n_x):
        disk = disk + swap(disk, "gy", 1)
        disks = [disk] + [
            swap_both(disk, a, b) for a in range(n_x) for b in range(0, n_y, 2) if (a, b) != (0, 0)
        ]
    else:
        disks = [swap_both(disk, a, b) for a in range(n_x) for b in range(n_y)]

    total_x, total_y = n_x * span_x, n_y * span_y
    solve_need = 4 * depth * ((total_x + 4) * (total_y + 16) * 6 + 8 * span_x * span_y) + 6 * MIB
    shared = max(ROOM - 4 * units * cells - MIB // 4, solve_need)
    whole = lambda shape: pl.BlockSpec(shape, lambda i: (0,) * len(shape))
    planes = 2
    chunk = planes * span_y * depth
    face_shape = [f.shape for f in faces]
    hidden_one, hidden_two, features, closure = pl.pallas_call(
        functools.partial(forward_kernel, plan, len(faces)),
        name="closure_forward",
        grid=(span_x // planes,),
        out_shape=(
            shape_of((units, cells), BF16),
            shape_of((units, cells), BF16),
            shape_of((16, cells), BF16),
            shape_of((3, span_x, span_y, depth), F32),
        ),
        in_specs=[whole(s) for s in face_shape]
        + [
            whole(v.shape),
            whole((feats, units)),
            whole((1, units)),
            whole(weight_mid.shape),
            whole((1, units)),
            whole(weight_out.shape),
            sspec(),
        ],
        out_specs=(
            pl.BlockSpec((units, chunk), lambda i: (0, i)),
            pl.BlockSpec((units, chunk), lambda i: (0, i)),
            pl.BlockSpec((16, chunk), lambda i: (0, i)),
            pl.BlockSpec((3, planes, span_y, depth), lambda i: (0, i, 0, 0)),
        ),
        scratch_shapes=[
            VMEM((3, span_x + 2, span_y + 16, depth), F32),
            VMEM((16 * planes * span_y, depth), F32),
            VMEM((8 * planes * span_y, depth), F32),
            VMEM((units, 16), BF16),
            VMEM((units, 8), F32),
            VMEM((16, chunk), BF16),
        ],
        compiler_params=pltpu.CompilerParams(vmem_limit_bytes=shared),
    )(*faces, v, stay(weight_in.T), stay(bias_in.reshape(1, units)), stay(weight_mid), stay(bias_mid.reshape(1, units)), stay(weight_out), stay(bias_out))

    basis, modes = (jnp.asarray(a) for a in depth_basis(depth))
    message = shape_of((span_x + 2, span_y, depth), F32)
    prov, first, second = pl.pallas_call(
        functools.partial(provisional_kernel, plan, len(faces), len(disks)),
        name="provisional",
        out_shape=(shape_of(v.shape, BF16), message, message),
        in_specs=[sspec()] + [vspec() for _ in range(len(faces) + len(disks) + 7)],
        out_specs=(vspec(), vspec(), vspec()),
        scratch_shapes=[
            VMEM((3, span_x + 2, span_y + 16, depth), F32),
            VMEM((span_x * span_y, depth), F32),
            VMEM((3, span_x + 2, span_y + 16, depth), F32),
            VMEM(message.shape, F32),
            VMEM(message.shape, F32),
        ],
        compiler_params=pltpu.CompilerParams(vmem_limit_bytes=shared),
    )(stay(tile_turbine), *faces, *disks, stay(tile_cells), stay(tile_weight), stay(thrust_coef.reshape(1, turbines)), v, t, closure, stay(basis))

    if is_power(n_x) and is_power(n_y):
        x_bits, y_bits = bits_of("gx", n_x), bits_of("gy", n_y)
        firsts = gather_doubling(first, x_bits + y_bits)
        seconds = gather_doubling(second, y_bits[:-1] + x_bits + y_bits[-1:])
    else:
        steps = [(a, b) for a in range(n_x) for b in range(n_y)]
        firsts = {s: swap_both(first, *s) for s in steps}
        seconds = {s: swap_both(second, *s) for s in steps}
    offsets = sorted(firsts)
    total_x, total_y = n_x * span_x, n_y * span_y
    new, force_field, cost = pl.pallas_call(
        functools.partial(solve_kernel, tuple(offsets), n_x, n_y),
        name="solve",
        out_shape=(shape_of(v.shape, BF16), shape_of(v.shape, BF16), shape_of((8, depth), F32)),
        in_specs=[vspec() for _ in range(2 * len(offsets) + 4)],
        out_specs=(vspec(), vspec(), vspec()),
        scratch_shapes=[
            VMEM((total_x + 2, total_y + 16, depth), F32),
            VMEM((total_x, total_y, depth), F32),
            VMEM((total_x, total_y, depth), F32),
            VMEM((total_x + 4, total_y + 16, depth), F32),
            VMEM((total_x + 4, total_y + 16, depth), F32),
            VMEM((3, span_x, span_y, depth), F32),
            VMEM((3, span_x * span_y, depth), F32),
            VMEM((total_x, total_y, depth), F32),
        ],
        compiler_params=pltpu.CompilerParams(vmem_limit_bytes=shared),
    )(*[firsts[o] for o in offsets], *[seconds[o] for o in offsets], prov, t, stay(basis), stay(modes))

    n_pieces = n_x * n_y
    total_rows = -(-(units + 32) // (8 * n_pieces)) * 8 * n_pieces
    paired = n_y > 1 and is_power(n_x) and is_power(n_y) and is_power(n_case)
    n_sums = 2 if paired else 1
    planes = 1
    chunk = planes * span_y * depth
    sums = pl.pallas_call(
        functools.partial(backward_kernel, n_sums),
        name="closure_backward",
        grid=(span_x // planes,),
        out_shape=(shape_of((total_rows // n_sums, units), F32),) * n_sums,
        in_specs=[
            pl.BlockSpec((3, planes, span_y, depth), lambda i: (0, i, 0, 0)),
            pl.BlockSpec((16, chunk), lambda i: (0, i)),
            pl.BlockSpec((units, chunk), lambda i: (0, i)),
            pl.BlockSpec((units, chunk), lambda i: (0, i)),
            whole(weight_out.shape),
            whole(weight_mid.shape),
            whole((8, depth)),
        ],
        out_specs=(whole((total_rows // n_sums, units)),) * n_sums,
        scratch_shapes=[
            VMEM((16 * planes * span_y, depth), F32),
            VMEM((units + 16, units), F32),
            VMEM((16, units), F32),
            VMEM((16, units), F32),
            VMEM((8, depth), F32),
            VMEM((units, 16), BF16),
            VMEM((units, units), BF16),
            VMEM((total_rows, units), F32),
        ],
        compiler_params=pltpu.CompilerParams(vmem_limit_bytes=shared),
    )(stay(force_field), features, hidden_one, hidden_two, stay(weight_out), stay(weight_mid), cost)

    if paired:
        group = n_pieces // 2
        size = total_rows // n_pieces
        mine = sums[0] + swap(sums[1], "gy", 1)
        steps = [(a, b) for a in range(n_x) for b in range(0, n_y, 2)]
        spot = lambda a, b: (ix ^ a) * (n_y // 2) + ((iy ^ b) >> 1)
        cut = lambda s: lax.dynamic_slice_in_dim(mine, spot(*s) * size, size, 0)
        piece = cut((0, 0))
        for s in steps[1:]:
            piece = piece + swap_both(cut(s), *s)
        for _, bit in reversed(bits_of("case", n_case)):
            piece = piece + swap(piece, "case", bit)
        here = [piece] + [swap_both(piece, *s) for s in steps[1:]]
        there = [swap(p, "gy", 1) for p in here]
        pieces = here + there

        def spot_of():
            jx, jy = lax.axis_index("gx"), lax.axis_index("gy")
            base = [(jx ^ a) * (n_y // 2) + ((jy ^ b) >> 1) for a, b in steps]
            return [(jy & 1) * group + k for k in base] + [(1 - (jy & 1)) * group + k for k in base]

    else:
        pieces = [lax.psum(sums[0], ("case", "gx", "gy"))]
        spot_of = lambda: [0]

    entry_total = units * feats + units + units * units + units + 3 * units + 3
    cell_total = 3 * cells * n_case * n_x * n_y
    loss, s_in, sb_in, s_mid, sb_mid, s_out, sb_out = pl.pallas_call(
        functools.partial(finish_kernel, spot_of, entry_total, cell_total),
        name="finish",
        out_shape=(
            shape_of((1, 1), F32),
            shape_of((feats, units), F32),
            shape_of((1, units), F32),
            shape_of((units, units), F32),
            shape_of((1, units), F32),
            shape_of((3, units), F32),
            shape_of((1, 3), F32),
        ),
        in_specs=[vspec() for _ in pieces],
        out_specs=tuple(vspec() for _ in range(7)),
        scratch_shapes=[VMEM((total_rows, units), F32)],
        compiler_params=pltpu.CompilerParams(vmem_limit_bytes=LIMIT),
    )(*pieces)
    return (
        new[None],
        loss.reshape(()),
        s_in.T,
        sb_in.reshape(units),
        s_mid,
        sb_mid.reshape(units),
        s_out,
        sb_out.reshape(3),
        force_field[None],
    )


def solution(mesh):
    placed = (
        P("case", None, "gx", "gy", None),
        P("case", None, "gx", "gy", None),
        P(),
        P(),
        P(),
        P(),
        P(),
        P(),
        P(),
        P(("gx", "gy"), None),
        P(("gx", "gy")),
        P(("gx", "gy"), None),
    )
    field = P("case", None, "gx", "gy", None)
    return jax.shard_map(
        on_device,
        mesh=mesh,
        in_specs=placed,
        out_specs=(field, P(), P(), P(), P(), P(), P(), P(), field),
        check_vma=False,
    )
```

profile of v0, /device:TPU:0, one launch (start us, length us, event | category | flops | bytes accessed | tf_op | source)
XLA Modules:
  0.0 116.5 jit_solution(14471106057950630404)
XLA Ops:
  0.6 2.2 %start.1 = (bf16[6,16,128]{2,1,0:T(8,128)(2,1)}, bf16[6,16,128]{2,1,0:T(8,128)(2,1)}, bf16[6,16,128]{2,1,0:T(8,128)(2,1)}, f32[8,100]{1,0:T(8,128)}) custom-call(s32[8,128]{1,0:T(8,128)} %refs_7_.1, s32[8]{0:T(128)} %turbine_ref.3, f32[8,128]{1,0:T(8,128)} %refs_8_.3, bf16[3,16,16,128]{3,2,1,0:T(8,128)(2,1)} %bitcast.16, bf16[3,16,16,128]{3,2,1,0:T(8,128)(2,1)} %bitcast.13), custom_call_target="tpu_custom_call" | custom-call | tf_op jit(solution)/shard_map/start/pallas_call | solution.py:604
  2.8 3.0 %collective-permute-start = (bf16[6,16,128]{2,1,0:T(8,128)(2,1)}, bf16[6,16,128]{2,1,0:T(8,128)(2,1)S(1)}, u32[]{:S(2)}, u32[]{:S(2)}) collective-permute-start(bf16[6,16,128]{2,1,0:T(8,128)(2,1)} %get-tuple-element.32), channel_id=1, source_target_pairs={{0,4},{4,0},{1,5},{5,1},{2,6},{6,2},{3,7},{7,3},{8,12},{12,8},{9,1... | collective-permute-start | bytes 73736 | tf_op jit(solution)/shard_map/ppermute | solution.py:617
  6.5 2.9 %collective-permute-start.3 = (f32[8,100]{1,0:T(8,128)}, f32[8,100]{1,0:T(8,128)S(1)}, u32[]{:S(2)}, u32[]{:S(2)}) collective-permute-start(f32[8,100]{1,0:T(8,128)} %get-tuple-element.35), channel_id=1, source_target_pairs={{0,1},{1,0},{2,3},{3,2},{4,5},{5,4},{6,7},{7,6},{8,9},{9,8},{10,11... | collective-permute-start | bytes 9608 | tf_op jit(solution)/shard_map/ppermute | solution.py:554
  9.4 1.0 collective-permute-done.3
  11.1 0.9 collective-permute-start.4
  12.0 2.6 %collective-permute-start.6 = (f32[8,100]{1,0:T(8,128)S(1)}, f32[8,100]{1,0:T(8,128)S(1)}, u32[]{:S(2)}, u32[]{:S(2)}) collective-permute-start(f32[8,100]{1,0:T(8,128)S(1)} %add.45.refs_3_), channel_id=1, source_target_pairs={{0,6},{1,7},{2,4},{3,5},{4,2},{5,3},{6,0},{7,1},{8,14},{9,15},{10,... | collective-permute-start | bytes 9608 | tf_op jit(solution)/shard_map/ppermute | solution.py:562
  14.6 16.0 %closure_forward.1 = (bf16[256,32768]{1,0:T(8,128)(2,1)S(1)}, bf16[256,32768]{1,0:T(8,128)(2,1)}, bf16[16,32768]{1,0:T(8,128)(2,1)S(1)}, f32[3,16,16,128]{3,2,1,0:T(8,128)S(1)}) custom-call(bf16[6,16,128]{2,1,0:T(8,128)(2,1)S(1)} %collective-permute-done.refs_0_, bf16[6,16,128]{2,1,0:T(8,128)(2,1)S(1)} %collective-permute-done.1.refs_1_, ...), custom_call_target="tpu_custom_call" | custom-call | tf_op jit(solution)/shard_map/closure_forward/pallas_call | solution.py:633
  30.6 2.9 %provisional.1 = (bf16[3,16,16,128]{3,2,1,0:T(8,128)(2,1)S(1)}, f32[18,16,128]{2,1,0:T(8,128)S(1)}, f32[18,16,128]{2,1,0:T(8,128)S(1)}) custom-call(s32[8]{0:T(128)} %turbine_ref.3, bf16[6,16,128]{2,1,0:T(8,128)(2,1)S(1)} %collective-permute-done.refs_0_, bf16[6,16,128]{2,1,0:T(8,128)(2,1)S(1)} %collective-permute-done.1.refs_1_, ...), custom_call_target="tpu_custom_call" | custom-call | tf_op jit(solution)/shard_map/provisional/pallas_call | solution.py:672
  34.5 1.9 %collective-permute-start.17 = (f32[18,16,128]{2,1,0:T(8,128)S(1)}, f32[18,16,128]{2,1,0:T(8,128)S(1)}, u32[]{:S(2)}, u32[]{:S(2)}) collective-permute-start(f32[18,16,128]{2,1,0:T(8,128)S(1)} %get-tuple-element.38.refs_8_), channel_id=1, source_target_pairs={{0,4},{4,0},{1,5},{5,1},{2,6},{6,2},{3,7},{7,3},{8,12},{12,8},{9,1... | collective-permute-start | bytes 442376 | tf_op jit(solution)/shard_map/ppermute | solution.py:554
  36.5 1.2 collective-permute-start.8
  37.6 2.7 %collective-permute-done.10.refs_4_ = f32[18,16,128]{2,1,0:T(8,128)S(1)} collective-permute-done((f32[18,16,128]{2,1,0:T(8,128)S(1)}, f32[18,16,128]{2,1,0:T(8,128)S(1)}, u32[]{:S(2)}, u32[]{:S(2)}) %collective-permute-start.10) | collective-permute-done | bytes 147488 | tf_op jit(solution)/shard_map/ppermute | solution.py:554
  41.1 0.9 collective-permute-done.17.refs_12_
  42.0 0.9 collective-permute-start.19
  43.4 3.1 %collective-permute-done.12.refs_6_ = f32[18,16,128]{2,1,0:T(8,128)S(1)} collective-permute-done((f32[18,16,128]{2,1,0:T(8,128)S(1)}, f32[18,16,128]{2,1,0:T(8,128)S(1)}, u32[]{:S(2)}, u32[]{:S(2)}) %collective-permute-start.12) | collective-permute-done | bytes 147488 | tf_op jit(solution)/shard_map/ppermute | solution.py:554
  48.7 13.2 %solve.1 = (bf16[3,16,16,128]{3,2,1,0:T(8,128)(2,1)}, bf16[3,16,16,128]{3,2,1,0:T(8,128)(2,1)}, f32[8,128]{1,0:T(8,128)S(1)}) custom-call(f32[18,16,128]{2,1,0:T(8,128)S(1)} %get-tuple-element.37.refs_0_, f32[18,16,128]{2,1,0:T(8,128)S(1)} %collective-permute-done.7.refs_1_, f32[18,16,128]{2,1,0:T(8,128)S(1)} %collective-permute-done.8.refs_2_, ...), custom_call_target="tpu_custom_call" | custom-call | tf_op jit(solution)/shard_map/solve/pallas_call | solution.py:698
  61.9 26.2 %closure_backward.1 = (f32[160,256]{1,0:T(8,128)S(1)}, f32[160,256]{1,0:T(8,128)S(1)}) custom-call(bf16[3,16,16,128]{3,2,1,0:T(8,128)(2,1)} %get-tuple-element.41.grad_ref, bf16[16,32768]{1,0:T(8,128)(2,1)S(1)} %get-tuple-element.42.feat_ref, bf16[256,32768]{1,0:T(8,128)(2,1)S(1)} %get-tuple-element.43.one_ref, ...), custom_call_target="tpu_custom_call" | custom-call | tf_op jit(solution)/shard_map/closure_backward/pallas_call | solution.py:723
  88.5 1.1 collective-permute-done.21
  89.6 1.2 %collective-permute-start.22 = (f32[40,256]{1,0:T(8,128)S(1)}, f32[40,256]{1,0:T(8,128)S(1)}, u32[]{:S(2)}, u32[]{:S(2)}) collective-permute-start(f32[40,256]{1,0:T(8,128)S(1)} %get-tuple-element.55), channel_id=1, source_target_pairs={{0,2},{1,3},{2,0},{3,1},{4,6},{5,7},{6,4},{7,5},{8,10},{9,11},{10,... | collective-permute-start | bytes 122888 | tf_op jit(solution)/shard_map/ppermute | solution.py:562
  90.9 1.0 collective-permute-start.23
  91.9 1.3 %collective-permute-start.24 = (f32[40,256]{1,0:T(8,128)S(1)}, f32[40,256]{1,0:T(8,128)S(1)}, u32[]{:S(2)}, u32[]{:S(2)}) collective-permute-start(f32[40,256]{1,0:T(8,128)S(1)} %get-tuple-element.56), channel_id=1, source_target_pairs={{0,6},{1,7},{2,4},{3,5},{4,2},{5,3},{6,0},{7,1},{8,14},{9,15},{10,... | collective-permute-start | bytes 122888 | tf_op jit(solution)/shard_map/ppermute | solution.py:562
  93.7 1.2 %collective-permute-done.23 = f32[40,256]{1,0:T(8,128)S(1)} collective-permute-done((f32[40,256]{1,0:T(8,128)S(1)}, f32[40,256]{1,0:T(8,128)S(1)}, u32[]{:S(2)}, u32[]{:S(2)}) %collective-permute-start.23) | collective-permute-done | bytes 40992 | tf_op jit(solution)/shard_map/ppermute | solution.py:562
  94.9 1.9 %collective-permute-done.24 = f32[40,256]{1,0:T(8,128)S(1)} collective-permute-done((f32[40,256]{1,0:T(8,128)S(1)}, f32[40,256]{1,0:T(8,128)S(1)}, u32[]{:S(2)}, u32[]{:S(2)}) %collective-permute-start.24) | collective-permute-done | bytes 40992 | tf_op jit(solution)/shard_map/ppermute | solution.py:562
  96.8 1.6 %collective-permute-start.25 = (f32[40,256]{1,0:T(8,128)S(1)}, f32[40,256]{1,0:T(8,128)S(1)}, u32[]{:S(2)}, u32[]{:S(2)}) collective-permute-start(f32[40,256]{1,0:T(8,128)S(1)} %add_add_fusion), channel_id=1, source_target_pairs={{0,8},{8,0},{16,24},{24,16},{1,9},{9,1},{17,25},{25,17},{2,10},{10... | collective-permute-start | bytes 122888 | tf_op jit(solution)/shard_map/ppermute | solution.py:554
  98.4 2.4 %collective-permute-done.25 = f32[40,256]{1,0:T(8,128)S(1)} collective-permute-done((f32[40,256]{1,0:T(8,128)S(1)}, f32[40,256]{1,0:T(8,128)S(1)}, u32[]{:S(2)}, u32[]{:S(2)}) %collective-permute-start.25) | collective-permute-done | bytes 40992 | tf_op jit(solution)/shard_map/ppermute | solution.py:554
  100.9 2.7 %collective-permute-start.26 = (f32[40,256]{1,0:T(8,128)S(1)}, f32[40,256]{1,0:T(8,128)S(1)}, u32[]{:S(2)}, u32[]{:S(2)}) collective-permute-start(f32[40,256]{1,0:T(8,128)S(1)} %add.58), channel_id=1, source_target_pairs={{0,16},{8,24},{16,0},{24,8},{1,17},{9,25},{17,1},{25,9},{2,18},{10... | collective-permute-start | bytes 122888 | tf_op jit(solution)/shard_map/ppermute | solution.py:554
  103.5 2.2 %collective-permute-done.26 = f32[40,256]{1,0:T(8,128)S(1)} collective-permute-done((f32[40,256]{1,0:T(8,128)S(1)}, f32[40,256]{1,0:T(8,128)S(1)}, u32[]{:S(2)}, u32[]{:S(2)}) %collective-permute-start.26) | collective-permute-done | bytes 40992 | tf_op jit(solution)/shard_map/ppermute | solution.py:554
  105.8 0.8 collective-permute-start.27
  106.5 1.2 collective-permute-start.28
  107.7 1.6 %collective-permute-start.29 = (f32[40,256]{1,0:T(8,128)S(1)}, f32[40,256]{1,0:T(8,128)S(1)}, u32[]{:S(2)}, u32[]{:S(2)}) collective-permute-start(f32[40,256]{1,0:T(8,128)S(1)} %add.59.refs_0_), channel_id=1, source_target_pairs={{0,6},{1,7},{2,4},{3,5},{4,2},{5,3},{6,0},{7,1},{8,14},{9,15},{10,... | collective-permute-start | bytes 122888 | tf_op jit(solution)/shard_map/ppermute | solution.py:562
  110.6 2.0 %collective-permute-done.29.refs_3_ = f32[40,256]{1,0:T(8,128)S(1)} collective-permute-done((f32[40,256]{1,0:T(8,128)S(1)}, f32[40,256]{1,0:T(8,128)S(1)}, u32[]{:S(2)}, u32[]{:S(2)}) %collective-permute-start.29) | collective-permute-done | bytes 40992 | tf_op jit(solution)/shard_map/ppermute | solution.py:562
  112.7 1.2 collective-permute-done.33.refs_7_
  114.5 2.0 %finish.1 = (f32[1,1]{1,0:T(1,128)}, f32[12,256]{1,0:T(8,128)}, f32[1,256]{1,0:T(1,128)}, f32[256,256]{1,0:T(8,128)}, f32[1,256]{1,0:T(1,128)}, /*index=5*/f32[3,256]{1,0:T(4,128)}, f32[1,3]{1,0:T(1,128)}) custom-call(f32[40,256]{1,0:T(8,128)} %copy-done, f32[40,256]{1,0:T(8,128)} %copy-done.1, f32[40,256]{1,0:T(8,128)} %copy-done.2, f32[40,256]{1,0:T(8,128)} %copy-done.3, ...), custom_call_target="tpu_custom_call" | custom-call | tf_op jit(solution)/shard_map/finish/pallas_call | solution.py:778
  (64 shorter events, 8.8 us)
Async XLA Ops:
  2.8 9.2 %collective-permute-start = (bf16[6,16,128]{2,1,0:T(8,128)(2,1)}, bf16[6,16,128]{2,1,0:T(8,128)(2,1)S(1)}, u32[]{:S(2)}, u32[]{:S(2)}) collective-permute-start(bf16[6,16,128]{2,1,0:T(8,128)(2,1)} %get-tuple-element.32), channel_id=1, source_target_pairs={{0,4},{4,0},{1,5},{5,1},{2,6},{6,2},{3,7},{7,3},{8,12},{12,8},{9,1... | collective-permute-start | bytes 73736 | tf_op jit(solution)/shard_map/ppermute | solution.py:617
  5.8 8.8 %collective-permute-start.1 = (bf16[6,16,128]{2,1,0:T(8,128)(2,1)}, bf16[6,16,128]{2,1,0:T(8,128)(2,1)S(1)}, u32[]{:S(2)}, u32[]{:S(2)}) collective-permute-start(bf16[6,16,128]{2,1,0:T(8,128)(2,1)} %get-tuple-element.33), channel_id=1, source_target_pairs={{0,1},{1,0},{2,3},{3,2},{4,5},{5,4},{6,7},{7,6},{8,9},{9,8},{10,11... | collective-permute-start | bytes 73736 | tf_op jit(solution)/shard_map/ppermute | solution.py:617
  5.8 8.8 %collective-permute-start.2 = (bf16[6,16,128]{2,1,0:T(8,128)(2,1)}, bf16[6,16,128]{2,1,0:T(8,128)(2,1)S(1)}, u32[]{:S(2)}, u32[]{:S(2)}) collective-permute-start(bf16[6,16,128]{2,1,0:T(8,128)(2,1)} %get-tuple-element.34), channel_id=1, source_target_pairs={{1,2},{2,1},{5,6},{6,5},{9,10},{10,9},{13,14},{14,13},{17,18},{18,... | collective-permute-start | bytes 73736 | tf_op jit(solution)/shard_map/ppermute | solution.py:617
  6.5 4.0 %collective-permute-start.3 = (f32[8,100]{1,0:T(8,128)}, f32[8,100]{1,0:T(8,128)S(1)}, u32[]{:S(2)}, u32[]{:S(2)}) collective-permute-start(f32[8,100]{1,0:T(8,128)} %get-tuple-element.35), channel_id=1, source_target_pairs={{0,1},{1,0},{2,3},{3,2},{4,5},{5,4},{6,7},{7,6},{8,9},{9,8},{10,11... | collective-permute-start | bytes 9608 | tf_op jit(solution)/shard_map/ppermute | solution.py:554
  11.1 19.5 %collective-permute-start.4 = (f32[8,100]{1,0:T(8,128)S(1)}, f32[8,100]{1,0:T(8,128)S(1)}, u32[]{:S(2)}, u32[]{:S(2)}) collective-permute-start(f32[8,100]{1,0:T(8,128)S(1)} %add.45.refs_3_), channel_id=1, source_target_pairs={{0,2},{1,3},{2,0},{3,1},{4,6},{5,7},{6,4},{7,5},{8,10},{9,11},{10,... | collective-permute-start | bytes 9608 | tf_op jit(solution)/shard_map/ppermute | solution.py:562
  12.0 18.6 %collective-permute-start.5 = (f32[8,100]{1,0:T(8,128)S(1)}, f32[8,100]{1,0:T(8,128)S(1)}, u32[]{:S(2)}, u32[]{:S(2)}) collective-permute-start(f32[8,100]{1,0:T(8,128)S(1)} %add.45.refs_3_), channel_id=1, source_target_pairs={{0,4},{1,5},{2,6},{3,7},{4,0},{5,1},{6,2},{7,3},{8,12},{9,13},{10,... | collective-permute-start | bytes 9608 | tf_op jit(solution)/shard_map/ppermute | solution.py:562
  12.0 18.6 %collective-permute-start.6 = (f32[8,100]{1,0:T(8,128)S(1)}, f32[8,100]{1,0:T(8,128)S(1)}, u32[]{:S(2)}, u32[]{:S(2)}) collective-permute-start(f32[8,100]{1,0:T(8,128)S(1)} %add.45.refs_3_), channel_id=1, source_target_pairs={{0,6},{1,7},{2,4},{3,5},{4,2},{5,3},{6,0},{7,1},{8,14},{9,15},{10,... | collective-permute-start | bytes 9608 | tf_op jit(solution)/shard_map/ppermute | solution.py:562
  33.5 6.8 %collective-permute-start.10 = (f32[18,16,128]{2,1,0:T(8,128)S(1)}, f32[18,16,128]{2,1,0:T(8,128)S(1)}, u32[]{:S(2)}, u32[]{:S(2)}) collective-permute-start(f32[18,16,128]{2,1,0:T(8,128)S(1)} %get-tuple-element.37.refs_0_), channel_id=1, source_target_pairs={{0,4},{4,0},{1,5},{5,1},{2,6},{6,2},{3,7},{7,3},{8,12},{12,8},{9,1... | collective-permute-start | bytes 442376 | tf_op jit(solution)/shard_map/ppermute | solution.py:554
  34.1 6.6 %collective-permute-start.15 = (f32[18,16,128]{2,1,0:T(8,128)S(1)}, f32[18,16,128]{2,1,0:T(8,128)S(1)}, u32[]{:S(2)}, u32[]{:S(2)}) collective-permute-start(f32[18,16,128]{2,1,0:T(8,128)S(1)} %get-tuple-element.38.refs_8_), channel_id=1, source_target_pairs={{0,2},{1,3},{2,0},{3,1},{4,6},{5,7},{6,4},{7,5},{8,10},{9,11},{10,... | collective-permute-start | bytes 442376 | tf_op jit(solution)/shard_map/ppermute | solution.py:554
  34.5 7.5 %collective-permute-start.17 = (f32[18,16,128]{2,1,0:T(8,128)S(1)}, f32[18,16,128]{2,1,0:T(8,128)S(1)}, u32[]{:S(2)}, u32[]{:S(2)}) collective-permute-start(f32[18,16,128]{2,1,0:T(8,128)S(1)} %get-tuple-element.38.refs_8_), channel_id=1, source_target_pairs={{0,4},{4,0},{1,5},{5,1},{2,6},{6,2},{3,7},{7,3},{8,12},{12,8},{9,1... | collective-permute-start | bytes 442376 | tf_op jit(solution)/shard_map/ppermute | solution.py:554
  36.5 6.4 %collective-permute-start.8 = (f32[18,16,128]{2,1,0:T(8,128)S(1)}, f32[18,16,128]{2,1,0:T(8,128)S(1)}, u32[]{:S(2)}, u32[]{:S(2)}) collective-permute-start(f32[18,16,128]{2,1,0:T(8,128)S(1)} %get-tuple-element.37.refs_0_), channel_id=1, source_target_pairs={{0,2},{1,3},{2,0},{3,1},{4,6},{5,7},{6,4},{7,5},{8,10},{9,11},{10,... | collective-permute-start | bytes 442376 | tf_op jit(solution)/shard_map/ppermute | solution.py:554
  37.6 5.2 %collective-permute-start.14 = (f32[18,16,128]{2,1,0:T(8,128)S(1)}, f32[18,16,128]{2,1,0:T(8,128)S(1)}, u32[]{:S(2)}, u32[]{:S(2)}) collective-permute-start(f32[18,16,128]{2,1,0:T(8,128)S(1)} %get-tuple-element.38.refs_8_), channel_id=1, source_target_pairs={{0,1},{1,0},{2,3},{3,2},{4,5},{5,4},{6,7},{7,6},{8,9},{9,8},{10,11... | collective-permute-start | bytes 442376 | tf_op jit(solution)/shard_map/ppermute | solution.py:554
  40.3 3.1 %collective-permute-start.7 = (f32[18,16,128]{2,1,0:T(8,128)S(1)}, f32[18,16,128]{2,1,0:T(8,128)S(1)}, u32[]{:S(2)}, u32[]{:S(2)}) collective-permute-start(f32[18,16,128]{2,1,0:T(8,128)S(1)} %get-tuple-element.37.refs_0_), channel_id=1, source_target_pairs={{0,1},{1,0},{2,3},{3,2},{4,5},{5,4},{6,7},{7,6},{8,9},{9,8},{10,11... | collective-permute-start | bytes 442376 | tf_op jit(solution)/shard_map/ppermute | solution.py:554
  40.7 5.8 %collective-permute-start.12 = (f32[18,16,128]{2,1,0:T(8,128)S(1)}, f32[18,16,128]{2,1,0:T(8,128)S(1)}, u32[]{:S(2)}, u32[]{:S(2)}) collective-permute-start(f32[18,16,128]{2,1,0:T(8,128)S(1)} %collective-permute-done.10.refs_4_), channel_id=1, source_target_pairs={{0,2},{1,3},{2,0},{3,1},{4,6},{5,7},{6,4},{7,5},{8,10},{9,11},{10,... | collective-permute-start | bytes 442376 | tf_op jit(solution)/shard_map/ppermute | solution.py:554
  42.0 5.1 %collective-permute-start.19 = (f32[18,16,128]{2,1,0:T(8,128)S(1)}, f32[18,16,128]{2,1,0:T(8,128)S(1)}, u32[]{:S(2)}, u32[]{:S(2)}) collective-permute-start(f32[18,16,128]{2,1,0:T(8,128)S(1)} %collective-permute-done.15.refs_10_), channel_id=1, source_target_pairs={{0,4},{4,0},{1,5},{5,1},{2,6},{6,2},{3,7},{7,3},{8,12},{12,8},{9,1... | collective-permute-start | bytes 442376 | tf_op jit(solution)/shard_map/ppermute | solution.py:554
  42.9 4.3 %collective-permute-start.11 = (f32[18,16,128]{2,1,0:T(8,128)S(1)}, f32[18,16,128]{2,1,0:T(8,128)S(1)}, u32[]{:S(2)}, u32[]{:S(2)}) collective-permute-start(f32[18,16,128]{2,1,0:T(8,128)S(1)} %collective-permute-done.10.refs_4_), channel_id=1, source_target_pairs={{0,1},{1,0},{2,3},{3,2},{4,5},{5,4},{6,7},{7,6},{8,9},{9,8},{10,11... | collective-permute-start | bytes 442376 | tf_op jit(solution)/shard_map/ppermute | solution.py:554
  42.9 4.8 %collective-permute-start.16 = (f32[18,16,128]{2,1,0:T(8,128)S(1)}, f32[18,16,128]{2,1,0:T(8,128)S(1)}, u32[]{:S(2)}, u32[]{:S(2)}) collective-permute-start(f32[18,16,128]{2,1,0:T(8,128)S(1)} %collective-permute-done.15.refs_10_), channel_id=1, source_target_pairs={{0,1},{1,0},{2,3},{3,2},{4,5},{5,4},{6,7},{7,6},{8,9},{9,8},{10,11... | collective-permute-start | bytes 442376 | tf_op jit(solution)/shard_map/ppermute | solution.py:554
  43.4 4.3 %collective-permute-start.18 = (f32[18,16,128]{2,1,0:T(8,128)S(1)}, f32[18,16,128]{2,1,0:T(8,128)S(1)}, u32[]{:S(2)}, u32[]{:S(2)}) collective-permute-start(f32[18,16,128]{2,1,0:T(8,128)S(1)} %collective-permute-done.17.refs_12_), channel_id=1, source_target_pairs={{0,1},{1,0},{2,3},{3,2},{4,5},{5,4},{6,7},{7,6},{8,9},{9,8},{10,11... | collective-permute-start | bytes 442376 | tf_op jit(solution)/shard_map/ppermute | solution.py:554
  46.6 1.4 %collective-permute-start.9 = (f32[18,16,128]{2,1,0:T(8,128)S(1)}, f32[18,16,128]{2,1,0:T(8,128)S(1)}, u32[]{:S(2)}, u32[]{:S(2)}) collective-permute-start(f32[18,16,128]{2,1,0:T(8,128)S(1)} %collective-permute-done.8.refs_2_), channel_id=1, source_target_pairs={{0,1},{1,0},{2,3},{3,2},{4,5},{5,4},{6,7},{7,6},{8,9},{9,8},{10,11... | collective-permute-start | bytes 442376 | tf_op jit(solution)/shard_map/ppermute | solution.py:554
  47.1 1.6 %collective-permute-start.20 = (f32[18,16,128]{2,1,0:T(8,128)S(1)}, f32[18,16,128]{2,1,0:T(8,128)S(1)}, u32[]{:S(2)}, u32[]{:S(2)}) collective-permute-start(f32[18,16,128]{2,1,0:T(8,128)S(1)} %collective-permute-done.19.refs_14_), channel_id=1, source_target_pairs={{0,1},{1,0},{2,3},{3,2},{4,5},{5,4},{6,7},{7,6},{8,9},{9,8},{10,11... | collective-permute-start | bytes 442376 | tf_op jit(solution)/shard_map/ppermute | solution.py:554
  88.1 1.5 %collective-permute-start.21 = (f32[160,256]{1,0:T(8,128)S(1)}, f32[160,256]{1,0:T(8,128)S(1)}, u32[]{:S(2)}, u32[]{:S(2)}) collective-permute-start(f32[160,256]{1,0:T(8,128)S(1)} %get-tuple-element.47), channel_id=1, source_target_pairs={{0,1},{1,0},{2,3},{3,2},{4,5},{5,4},{6,7},{7,6},{8,9},{9,8},{10,11... | collective-permute-start | bytes 491528 | tf_op jit(solution)/shard_map/ppermute | solution.py:554
  89.6 4.1 %collective-permute-start.22 = (f32[40,256]{1,0:T(8,128)S(1)}, f32[40,256]{1,0:T(8,128)S(1)}, u32[]{:S(2)}, u32[]{:S(2)}) collective-permute-start(f32[40,256]{1,0:T(8,128)S(1)} %get-tuple-element.55), channel_id=1, source_target_pairs={{0,2},{1,3},{2,0},{3,1},{4,6},{5,7},{6,4},{7,5},{8,10},{9,11},{10,... | collective-permute-start | bytes 122888 | tf_op jit(solution)/shard_map/ppermute | solution.py:562
  90.9 4.0 %collective-permute-start.23 = (f32[40,256]{1,0:T(8,128)S(1)}, f32[40,256]{1,0:T(8,128)S(1)}, u32[]{:S(2)}, u32[]{:S(2)}) collective-permute-start(f32[40,256]{1,0:T(8,128)S(1)} %get-tuple-element.57), channel_id=1, source_target_pairs={{0,4},{1,5},{2,6},{3,7},{4,0},{5,1},{6,2},{7,3},{8,12},{9,13},{10,... | collective-permute-start | bytes 122888 | tf_op jit(solution)/shard_map/ppermute | solution.py:562
  91.9 4.9 %collective-permute-start.24 = (f32[40,256]{1,0:T(8,128)S(1)}, f32[40,256]{1,0:T(8,128)S(1)}, u32[]{:S(2)}, u32[]{:S(2)}) collective-permute-start(f32[40,256]{1,0:T(8,128)S(1)} %get-tuple-element.56), channel_id=1, source_target_pairs={{0,6},{1,7},{2,4},{3,5},{4,2},{5,3},{6,0},{7,1},{8,14},{9,15},{10,... | collective-permute-start | bytes 122888 | tf_op jit(solution)/shard_map/ppermute | solution.py:562
  96.8 4.1 %collective-permute-start.25 = (f32[40,256]{1,0:T(8,128)S(1)}, f32[40,256]{1,0:T(8,128)S(1)}, u32[]{:S(2)}, u32[]{:S(2)}) collective-permute-start(f32[40,256]{1,0:T(8,128)S(1)} %add_add_fusion), channel_id=1, source_target_pairs={{0,8},{8,0},{16,24},{24,16},{1,9},{9,1},{17,25},{25,17},{2,10},{10... | collective-permute-start | bytes 122888 | tf_op jit(solution)/shard_map/ppermute | solution.py:554
  100.9 4.9 %collective-permute-start.26 = (f32[40,256]{1,0:T(8,128)S(1)}, f32[40,256]{1,0:T(8,128)S(1)}, u32[]{:S(2)}, u32[]{:S(2)}) collective-permute-start(f32[40,256]{1,0:T(8,128)S(1)} %add.58), channel_id=1, source_target_pairs={{0,16},{8,24},{16,0},{24,8},{1,17},{9,25},{17,1},{25,9},{2,18},{10... | collective-permute-start | bytes 122888 | tf_op jit(solution)/shard_map/ppermute | solution.py:554
  105.8 4.1 %collective-permute-start.27 = (f32[40,256]{1,0:T(8,128)S(1)}, f32[40,256]{1,0:T(8,128)S(1)}, u32[]{:S(2)}, u32[]{:S(2)}) collective-permute-start(f32[40,256]{1,0:T(8,128)S(1)} %add.59.refs_0_), channel_id=1, source_target_pairs={{0,2},{1,3},{2,0},{3,1},{4,6},{5,7},{6,4},{7,5},{8,10},{9,11},{10,... | collective-permute-start | bytes 122888 | tf_op jit(solution)/shard_map/ppermute | solution.py:562
  106.5 4.0 %collective-permute-start.28 = (f32[40,256]{1,0:T(8,128)S(1)}, f32[40,256]{1,0:T(8,128)S(1)}, u32[]{:S(2)}, u32[]{:S(2)}) collective-permute-start(f32[40,256]{1,0:T(8,128)S(1)} %add.59.refs_0_), channel_id=1, source_target_pairs={{0,4},{1,5},{2,6},{3,7},{4,0},{5,1},{6,2},{7,3},{8,12},{9,13},{10,... | collective-permute-start | bytes 122888 | tf_op jit(solution)/shard_map/ppermute | solution.py:562
  107.7 4.9 %collective-permute-start.29 = (f32[40,256]{1,0:T(8,128)S(1)}, f32[40,256]{1,0:T(8,128)S(1)}, u32[]{:S(2)}, u32[]{:S(2)}) collective-permute-start(f32[40,256]{1,0:T(8,128)S(1)} %add.59.refs_0_), channel_id=1, source_target_pairs={{0,6},{1,7},{2,4},{3,5},{4,2},{5,3},{6,0},{7,1},{8,14},{9,15},{10,... | collective-permute-start | bytes 122888 | tf_op jit(solution)/shard_map/ppermute | solution.py:562
  109.3 3.3 %collective-permute-start.30 = (f32[40,256]{1,0:T(8,128)S(1)}, f32[40,256]{1,0:T(8,128)S(1)}, u32[]{:S(2)}, u32[]{:S(2)}) collective-permute-start(f32[40,256]{1,0:T(8,128)S(1)} %add.59.refs_0_), channel_id=1, source_target_pairs={{0,1},{1,0},{2,3},{3,2},{4,5},{5,4},{6,7},{7,6},{8,9},{9,8},{10,11... | collective-permute-start | bytes 122888 | tf_op jit(solution)/shard_map/ppermute | solution.py:554
  109.9 2.8 %collective-permute-start.31 = (f32[40,256]{1,0:T(8,128)S(1)}, f32[40,256]{1,0:T(8,128)S(1)}, u32[]{:S(2)}, u32[]{:S(2)}) collective-permute-start(f32[40,256]{1,0:T(8,128)S(1)} %collective-permute-done.27.refs_1_), channel_id=1, source_target_pairs={{0,1},{1,0},{2,3},{3,2},{4,5},{5,4},{6,7},{7,6},{8,9},{9,8},{10,11... | collective-permute-start | bytes 122888 | tf_op jit(solution)/shard_map/ppermute | solution.py:554
  110.5 2.1 %collective-permute-start.32 = (f32[40,256]{1,0:T(8,128)S(1)}, f32[40,256]{1,0:T(8,128)S(1)}, u32[]{:S(2)}, u32[]{:S(2)}) collective-permute-start(f32[40,256]{1,0:T(8,128)S(1)} %collective-permute-done.28.refs_2_), channel_id=1, source_target_pairs={{0,1},{1,0},{2,3},{3,2},{4,5},{5,4},{6,7},{7,6},{8,9},{9,8},{10,11... | collective-permute-start | bytes 122888 | tf_op jit(solution)/shard_map/ppermute | solution.py:554
  (10 other events, 23.4 us)
where the time goes:
time: 117 us; the launch traced here: 116 us
  Pallas kernels  62.4 us (53%)
  starting transfers between devices  28.3 us (24%)
  waiting for transfers between devices  23.5 us (20%)
    pallas_call x1, Pallas kernels, on_device(): pl.pallas_call(functools.partial(backward_kernel, n_sums), name='closure_...  26.2 us
    ppermute x22, waiting for transfers between devices, swap(): lax.ppermute(values, axis, [(i, partner(i, step, count)) for i in range(c...  16.7 us
    pallas_call x1, Pallas kernels, on_device(): pl.pallas_call(functools.partial(forward_kernel, plan, len(faces)), name=...  16 us
    ppermute x22, starting transfers between devices, swap(): lax.ppermute(values, axis, [(i, partner(i, step, count)) for i in range(c...  14.1 us
    pallas_call x1, Pallas kernels, on_device(): pl.pallas_call(functools.partial(solve_kernel, tuple(offsets), n_x, n_y),...  13.2 us
    ppermute x9, starting transfers between devices, swap_both(): return lax.ppermute(values, ('gx', 'gy'), pairs)  10.6 us
    ppermute x9, waiting for transfers between devices, swap_both(): return lax.ppermute(values, ('gx', 'gy'), pairs)  6.87 us
    ppermute x3, starting transfers between devices, on_device(): faces.append(lax.ppermute(face, axis, pair_list(count, parity)))  3.65 us
  transfers between devices with their start and end apart: 34, of which 19 were waited for; matrix products, arithmetic and copies ran while one was open for 1% of the time, Pallas kernels for 14%

commit v1 on v0

--- a/solution.py
+++ b/solution.py
@@ -608,8 +608,8 @@
         + (shape_of((8, turbines), F32),),
         in_specs=[vspec(), sspec(), vspec(), vspec(), vspec()],
         out_specs=tuple(vspec() for _ in range(len(plan) + 1)),
-        compiler_params=pltpu.CompilerParams(vmem_limit_bytes=LIMIT),
-    )(tile_cells, tile_turbine, tile_weight, v, t)
+        compiler_params=pltpu.CompilerParams(vmem_limit_bytes=24 * MIB),
+    )(stay(tile_cells), stay(tile_turbine), stay(tile_weight), v, t)
     disk = started[-1]
     faces = []
     for face, (dim, parity) in zip(started[:-1], plan):
@@ -790,7 +790,7 @@
         in_specs=[vspec() for _ in pieces],
         out_specs=tuple(vspec() for _ in range(7)),
         scratch_shapes=[VMEM((total_rows, units), F32)],
-        compiler_params=pltpu.CompilerParams(vmem_limit_bytes=LIMIT),
+        compiler_params=pltpu.CompilerParams(vmem_limit_bytes=8 * MIB),
     )(*pieces)
     return (
         new[None],

time: 117 us -> 114 us (0.974)
  Pallas kernels: 62.4 us -> 60.9 us
  transfers between devices with their start and end apart: 34 -> 34, of which waited for: 19 -> 19; matrix products, arithmetic and copies ran while one was open for 1% -> 0% of each run, Pallas kernels for 14% -> 14%
where the time goes in v1:
time: 114 us; the launch traced here: 113 us
  Pallas kernels  60.9 us (53%)
  starting transfers between devices  28.3 us (25%)
  waiting for transfers between devices  23.4 us (21%)
    pallas_call x1, Pallas kernels, on_device(): pl.pallas_call(functools.partial(backward_kernel, n_sums), name='closure_...  26.2 us
    ppermute x22, waiting for transfers between devices, swap(): lax.ppermute(values, axis, [(i, partner(i, step, count)) for i in range(c...  16.6 us
    pallas_call x1, Pallas kernels, on_device(): pl.pallas_call(functools.partial(forward_kernel, plan, len(faces)), name=...  16 us
    ppermute x22, starting transfers between devices, swap(): lax.ppermute(values, axis, [(i, partner(i, step, count)) for i in range(c...  14 us
    pallas_call x1, Pallas kernels, on_device(): pl.pallas_call(functools.partial(solve_kernel, tuple(offsets), n_x, n_y),...  13.2 us
    ppermute x9, starting transfers between devices, swap_both(): return lax.ppermute(values, ('gx', 'gy'), pairs)  10.5 us
    ppermute x9, waiting for transfers between devices, swap_both(): return lax.ppermute(values, ('gx', 'gy'), pairs)  6.87 us
    ppermute x3, starting transfers between devices, on_device(): faces.append(lax.ppermute(face, axis, pair_list(count, parity)))  3.71 us
  transfers between devices with their start and end apart: 34, of which 19 were waited for; matrix products, arithmetic and copies ran while one was open for 0% of the time, Pallas kernels for 14%

profile of v1, /device:TPU:0, one launch (start us, length us, event | category | flops | bytes accessed | tf_op | source)
XLA Modules:
  0.0 113.5 jit_solution(15511697697632419092)
XLA Ops:
  0.6 1.6 %start.1 = (bf16[6,16,128]{2,1,0:T(8,128)(2,1)S(1)}, bf16[6,16,128]{2,1,0:T(8,128)(2,1)S(1)}, bf16[6,16,128]{2,1,0:T(8,128)(2,1)S(1)}, f32[8,100]{1,0:T(8,128)S(1)}) custom-call(s32[8,128]{1,0:T(8,128)} %refs_7_.1, s32[8]{0:T(128)} %turbine_ref.3, f32[8,128]{1,0:T(8,128)} %refs_8_.3, bf16[3,16,16,128]{3,2,1,0:T(8,128)(2,1)} %bitcast.16, ...), custom_call_target="tpu_custom_call" | custom-call | tf_op jit(solution)/shard_map/start/pallas_call | solution.py:604
  2.3 3.1 %collective-permute-start = (bf16[6,16,128]{2,1,0:T(8,128)(2,1)S(1)}, bf16[6,16,128]{2,1,0:T(8,128)(2,1)S(1)}, u32[]{:S(2)}, u32[]{:S(2)}) collective-permute-start(bf16[6,16,128]{2,1,0:T(8,128)(2,1)S(1)} %get-tuple-element.32), channel_id=1, source_target_pairs={{0,4},{4,0},{1,5},{5,1},{2,6},{6,2},{3,7},{7,3},{8,12},{12,8},{9,1... | collective-permute-start | bytes 73736 | tf_op jit(solution)/shard_map/ppermute | solution.py:617
  6.0 2.9 %collective-permute-start.3 = (f32[8,100]{1,0:T(8,128)S(1)}, f32[8,100]{1,0:T(8,128)S(1)}, u32[]{:S(2)}, u32[]{:S(2)}) collective-permute-start(f32[8,100]{1,0:T(8,128)S(1)} %get-tuple-element.35), channel_id=1, source_target_pairs={{0,1},{1,0},{2,3},{3,2},{4,5},{5,4},{6,7},{7,6},{8,9},{9,8},{10,11... | collective-permute-start | bytes 9608 | tf_op jit(solution)/shard_map/ppermute | solution.py:554
  8.9 0.8 collective-permute-done.3
  9.8 0.9 collective-permute-start.4
  10.7 2.5 %collective-permute-start.6 = (f32[8,100]{1,0:T(8,128)S(1)}, f32[8,100]{1,0:T(8,128)S(1)}, u32[]{:S(2)}, u32[]{:S(2)}) collective-permute-start(f32[8,100]{1,0:T(8,128)S(1)} %add.45.refs_3_), channel_id=1, source_target_pairs={{0,6},{1,7},{2,4},{3,5},{4,2},{5,3},{6,0},{7,1},{8,14},{9,15},{10,... | collective-permute-start | bytes 9608 | tf_op jit(solution)/shard_map/ppermute | solution.py:562
  13.3 16.0 %closure_forward.1 = (bf16[256,32768]{1,0:T(8,128)(2,1)S(1)}, bf16[256,32768]{1,0:T(8,128)(2,1)}, bf16[16,32768]{1,0:T(8,128)(2,1)S(1)}, f32[3,16,16,128]{3,2,1,0:T(8,128)S(1)}) custom-call(bf16[6,16,128]{2,1,0:T(8,128)(2,1)S(1)} %collective-permute-done.refs_0_, bf16[6,16,128]{2,1,0:T(8,128)(2,1)S(1)} %collective-permute-done.1.refs_1_, ...), custom_call_target="tpu_custom_call" | custom-call | tf_op jit(solution)/shard_map/closure_forward/pallas_call | solution.py:633
  29.3 2.8 %provisional.1 = (bf16[3,16,16,128]{3,2,1,0:T(8,128)(2,1)S(1)}, f32[18,16,128]{2,1,0:T(8,128)S(1)}, f32[18,16,128]{2,1,0:T(8,128)S(1)}) custom-call(s32[8]{0:T(128)} %turbine_ref.3, bf16[6,16,128]{2,1,0:T(8,128)(2,1)S(1)} %collective-permute-done.refs_0_, bf16[6,16,128]{2,1,0:T(8,128)(2,1)S(1)} %collective-permute-done.1.refs_1_, ...), custom_call_target="tpu_custom_call" | custom-call | tf_op jit(solution)/shard_map/provisional/pallas_call | solution.py:672
  33.2 1.9 %collective-permute-start.17 = (f32[18,16,128]{2,1,0:T(8,128)S(1)}, f32[18,16,128]{2,1,0:T(8,128)S(1)}, u32[]{:S(2)}, u32[]{:S(2)}) collective-permute-start(f32[18,16,128]{2,1,0:T(8,128)S(1)} %get-tuple-element.38.refs_8_), channel_id=1, source_target_pairs={{0,4},{4,0},{1,5},{5,1},{2,6},{6,2},{3,7},{7,3},{8,12},{12,8},{9,1... | collective-permute-start | bytes 442376 | tf_op jit(solution)/shard_map/ppermute | solution.py:554
  35.1 1.1 %collective-permute-start.8 = (f32[18,16,128]{2,1,0:T(8,128)S(1)}, f32[18,16,128]{2,1,0:T(8,128)S(1)}, u32[]{:S(2)}, u32[]{:S(2)}) collective-permute-start(f32[18,16,128]{2,1,0:T(8,128)S(1)} %get-tuple-element.37.refs_0_), channel_id=1, source_target_pairs={{0,2},{1,3},{2,0},{3,1},{4,6},{5,7},{6,4},{7,5},{8,10},{9,11},{10,... | collective-permute-start | bytes 442376 | tf_op jit(solution)/shard_map/ppermute | solution.py:554
  36.3 2.7 %collective-permute-done.10.refs_4_ = f32[18,16,128]{2,1,0:T(8,128)S(1)} collective-permute-done((f32[18,16,128]{2,1,0:T(8,128)S(1)}, f32[18,16,128]{2,1,0:T(8,128)S(1)}, u32[]{:S(2)}, u32[]{:S(2)}) %collective-permute-start.10) | collective-permute-done | bytes 147488 | tf_op jit(solution)/shard_map/ppermute | solution.py:554
  39.8 0.9 collective-permute-done.17.refs_12_
  40.6 0.9 collective-permute-start.19
  42.1 3.1 %collective-permute-done.12.refs_6_ = f32[18,16,128]{2,1,0:T(8,128)S(1)} collective-permute-done((f32[18,16,128]{2,1,0:T(8,128)S(1)}, f32[18,16,128]{2,1,0:T(8,128)S(1)}, u32[]{:S(2)}, u32[]{:S(2)}) %collective-permute-start.12) | collective-permute-done | bytes 147488 | tf_op jit(solution)/shard_map/ppermute | solution.py:554
  47.4 13.2 %solve.1 = (bf16[3,16,16,128]{3,2,1,0:T(8,128)(2,1)}, bf16[3,16,16,128]{3,2,1,0:T(8,128)(2,1)}, f32[8,128]{1,0:T(8,128)S(1)}) custom-call(f32[18,16,128]{2,1,0:T(8,128)S(1)} %get-tuple-element.37.refs_0_, f32[18,16,128]{2,1,0:T(8,128)S(1)} %collective-permute-done.7.refs_1_, f32[18,16,128]{2,1,0:T(8,128)S(1)} %collective-permute-done.8.refs_2_, ...), custom_call_target="tpu_custom_call" | custom-call | tf_op jit(solution)/shard_map/solve/pallas_call | solution.py:698
  60.6 26.2 %closure_backward.1 = (f32[160,256]{1,0:T(8,128)S(1)}, f32[160,256]{1,0:T(8,128)S(1)}) custom-call(bf16[3,16,16,128]{3,2,1,0:T(8,128)(2,1)} %get-tuple-element.41.grad_ref, bf16[16,32768]{1,0:T(8,128)(2,1)S(1)} %get-tuple-element.42.feat_ref, bf16[256,32768]{1,0:T(8,128)(2,1)S(1)} %get-tuple-element.43.one_ref, ...), custom_call_target="tpu_custom_call" | custom-call | tf_op jit(solution)/shard_map/closure_backward/pallas_call | solution.py:723
  87.2 1.1 collective-permute-done.21
  88.3 1.2 %collective-permute-start.22 = (f32[40,256]{1,0:T(8,128)S(1)}, f32[40,256]{1,0:T(8,128)S(1)}, u32[]{:S(2)}, u32[]{:S(2)}) collective-permute-start(f32[40,256]{1,0:T(8,128)S(1)} %get-tuple-element.55), channel_id=1, source_target_pairs={{0,2},{1,3},{2,0},{3,1},{4,6},{5,7},{6,4},{7,5},{8,10},{9,11},{10,... | collective-permute-start | bytes 122888 | tf_op jit(solution)/shard_map/ppermute | solution.py:562
  89.5 1.0 collective-permute-start.23
  90.5 1.3 %collective-permute-start.24 = (f32[40,256]{1,0:T(8,128)S(1)}, f32[40,256]{1,0:T(8,128)S(1)}, u32[]{:S(2)}, u32[]{:S(2)}) collective-permute-start(f32[40,256]{1,0:T(8,128)S(1)} %get-tuple-element.56), channel_id=1, source_target_pairs={{0,6},{1,7},{2,4},{3,5},{4,2},{5,3},{6,0},{7,1},{8,14},{9,15},{10,... | collective-permute-start | bytes 122888 | tf_op jit(solution)/shard_map/ppermute | solution.py:562
  92.3 1.2 %collective-permute-done.23 = f32[40,256]{1,0:T(8,128)S(1)} collective-permute-done((f32[40,256]{1,0:T(8,128)S(1)}, f32[40,256]{1,0:T(8,128)S(1)}, u32[]{:S(2)}, u32[]{:S(2)}) %collective-permute-start.23) | collective-permute-done | bytes 40992 | tf_op jit(solution)/shard_map/ppermute | solution.py:562
  93.5 1.9 %collective-permute-done.24 = f32[40,256]{1,0:T(8,128)S(1)} collective-permute-done((f32[40,256]{1,0:T(8,128)S(1)}, f32[40,256]{1,0:T(8,128)S(1)}, u32[]{:S(2)}, u32[]{:S(2)}) %collective-permute-start.24) | collective-permute-done | bytes 40992 | tf_op jit(solution)/shard_map/ppermute | solution.py:562
  95.5 1.6 %collective-permute-start.25 = (f32[40,256]{1,0:T(8,128)S(1)}, f32[40,256]{1,0:T(8,128)S(1)}, u32[]{:S(2)}, u32[]{:S(2)}) collective-permute-start(f32[40,256]{1,0:T(8,128)S(1)} %add_add_fusion), channel_id=1, source_target_pairs={{0,8},{8,0},{16,24},{24,16},{1,9},{9,1},{17,25},{25,17},{2,10},{10... | collective-permute-start | bytes 122888 | tf_op jit(solution)/shard_map/ppermute | solution.py:554
  97.1 2.4 %collective-permute-done.25 = f32[40,256]{1,0:T(8,128)S(1)} collective-permute-done((f32[40,256]{1,0:T(8,128)S(1)}, f32[40,256]{1,0:T(8,128)S(1)}, u32[]{:S(2)}, u32[]{:S(2)}) %collective-permute-start.25) | collective-permute-done | bytes 40992 | tf_op jit(solution)/shard_map/ppermute | solution.py:554
  99.5 2.6 %collective-permute-start.26 = (f32[40,256]{1,0:T(8,128)S(1)}, f32[40,256]{1,0:T(8,128)S(1)}, u32[]{:S(2)}, u32[]{:S(2)}) collective-permute-start(f32[40,256]{1,0:T(8,128)S(1)} %add.58), channel_id=1, source_target_pairs={{0,16},{8,24},{16,0},{24,8},{1,17},{9,25},{17,1},{25,9},{2,18},{10... | collective-permute-start | bytes 122888 | tf_op jit(solution)/shard_map/ppermute | solution.py:554
  102.1 2.3 %collective-permute-done.26 = f32[40,256]{1,0:T(8,128)S(1)} collective-permute-done((f32[40,256]{1,0:T(8,128)S(1)}, f32[40,256]{1,0:T(8,128)S(1)}, u32[]{:S(2)}, u32[]{:S(2)}) %collective-permute-start.26) | collective-permute-done | bytes 40992 | tf_op jit(solution)/shard_map/ppermute | solution.py:554
  104.4 0.7 collective-permute-start.27
  105.1 1.2 %collective-permute-start.28 = (f32[40,256]{1,0:T(8,128)S(1)}, f32[40,256]{1,0:T(8,128)S(1)}, u32[]{:S(2)}, u32[]{:S(2)}) collective-permute-start(f32[40,256]{1,0:T(8,128)S(1)} %add.59.refs_0_), channel_id=1, source_target_pairs={{0,4},{1,5},{2,6},{3,7},{4,0},{5,1},{6,2},{7,3},{8,12},{9,13},{10,... | collective-permute-start | bytes 122888 | tf_op jit(solution)/shard_map/ppermute | solution.py:562
  106.3 1.6 %collective-permute-start.29 = (f32[40,256]{1,0:T(8,128)S(1)}, f32[40,256]{1,0:T(8,128)S(1)}, u32[]{:S(2)}, u32[]{:S(2)}) collective-permute-start(f32[40,256]{1,0:T(8,128)S(1)} %add.59.refs_0_), channel_id=1, source_target_pairs={{0,6},{1,7},{2,4},{3,5},{4,2},{5,3},{6,0},{7,1},{8,14},{9,15},{10,... | collective-permute-start | bytes 122888 | tf_op jit(solution)/shard_map/ppermute | solution.py:562
  109.1 2.1 %collective-permute-done.29.refs_3_ = f32[40,256]{1,0:T(8,128)S(1)} collective-permute-done((f32[40,256]{1,0:T(8,128)S(1)}, f32[40,256]{1,0:T(8,128)S(1)}, u32[]{:S(2)}, u32[]{:S(2)}) %collective-permute-start.29) | collective-permute-done | bytes 40992 | tf_op jit(solution)/shard_map/ppermute | solution.py:562
  111.2 1.2 %collective-permute-done.33.refs_7_ = f32[40,256]{1,0:T(8,128)S(1)} collective-permute-done((f32[40,256]{1,0:T(8,128)S(1)}, f32[40,256]{1,0:T(8,128)S(1)}, u32[]{:S(2)}, u32[]{:S(2)}) %collective-permute-start.33) | collective-permute-done | bytes 40992 | tf_op jit(solution)/shard_map/ppermute | solution.py:554
  112.4 1.1 finish.1
  (48 shorter events, 7.5 us)
Async XLA Ops:
  2.3 8.4 %collective-permute-start = (bf16[6,16,128]{2,1,0:T(8,128)(2,1)S(1)}, bf16[6,16,128]{2,1,0:T(8,128)(2,1)S(1)}, u32[]{:S(2)}, u32[]{:S(2)}) collective-permute-start(bf16[6,16,128]{2,1,0:T(8,128)(2,1)S(1)} %get-tuple-element.32), channel_id=1, source_target_pairs={{0,4},{4,0},{1,5},{5,1},{2,6},{6,2},{3,7},{7,3},{8,12},{12,8},{9,1... | collective-permute-start | bytes 73736 | tf_op jit(solution)/shard_map/ppermute | solution.py:617
  5.4 7.9 %collective-permute-start.1 = (bf16[6,16,128]{2,1,0:T(8,128)(2,1)S(1)}, bf16[6,16,128]{2,1,0:T(8,128)(2,1)S(1)}, u32[]{:S(2)}, u32[]{:S(2)}) collective-permute-start(bf16[6,16,128]{2,1,0:T(8,128)(2,1)S(1)} %get-tuple-element.33), channel_id=1, source_target_pairs={{0,1},{1,0},{2,3},{3,2},{4,5},{5,4},{6,7},{7,6},{8,9},{9,8},{10,11... | collective-permute-start | bytes 73736 | tf_op jit(solution)/shard_map/ppermute | solution.py:617
  5.4 7.9 %collective-permute-start.2 = (bf16[6,16,128]{2,1,0:T(8,128)(2,1)S(1)}, bf16[6,16,128]{2,1,0:T(8,128)(2,1)S(1)}, u32[]{:S(2)}, u32[]{:S(2)}) collective-permute-start(bf16[6,16,128]{2,1,0:T(8,128)(2,1)S(1)} %get-tuple-element.34), channel_id=1, source_target_pairs={{1,2},{2,1},{5,6},{6,5},{9,10},{10,9},{13,14},{14,13},{17,18},{18,... | collective-permute-start | bytes 73736 | tf_op jit(solution)/shard_map/ppermute | solution.py:617
  6.0 3.7 %collective-permute-start.3 = (f32[8,100]{1,0:T(8,128)S(1)}, f32[8,100]{1,0:T(8,128)S(1)}, u32[]{:S(2)}, u32[]{:S(2)}) collective-permute-start(f32[8,100]{1,0:T(8,128)S(1)} %get-tuple-element.35), channel_id=1, source_target_pairs={{0,1},{1,0},{2,3},{3,2},{4,5},{5,4},{6,7},{7,6},{8,9},{9,8},{10,11... | collective-permute-start | bytes 9608 | tf_op jit(solution)/shard_map/ppermute | solution.py:554
  9.8 19.5 %collective-permute-start.4 = (f32[8,100]{1,0:T(8,128)S(1)}, f32[8,100]{1,0:T(8,128)S(1)}, u32[]{:S(2)}, u32[]{:S(2)}) collective-permute-start(f32[8,100]{1,0:T(8,128)S(1)} %add.45.refs_3_), channel_id=1, source_target_pairs={{0,2},{1,3},{2,0},{3,1},{4,6},{5,7},{6,4},{7,5},{8,10},{9,11},{10,... | collective-permute-start | bytes 9608 | tf_op jit(solution)/shard_map/ppermute | solution.py:562
  10.6 18.6 %collective-permute-start.5 = (f32[8,100]{1,0:T(8,128)S(1)}, f32[8,100]{1,0:T(8,128)S(1)}, u32[]{:S(2)}, u32[]{:S(2)}) collective-permute-start(f32[8,100]{1,0:T(8,128)S(1)} %add.45.refs_3_), channel_id=1, source_target_pairs={{0,4},{1,5},{2,6},{3,7},{4,0},{5,1},{6,2},{7,3},{8,12},{9,13},{10,... | collective-permute-start | bytes 9608 | tf_op jit(solution)/shard_map/ppermute | solution.py:562
  10.7 18.6 %collective-permute-start.6 = (f32[8,100]{1,0:T(8,128)S(1)}, f32[8,100]{1,0:T(8,128)S(1)}, u32[]{:S(2)}, u32[]{:S(2)}) collective-permute-start(f32[8,100]{1,0:T(8,128)S(1)} %add.45.refs_3_), channel_id=1, source_target_pairs={{0,6},{1,7},{2,4},{3,5},{4,2},{5,3},{6,0},{7,1},{8,14},{9,15},{10,... | collective-permute-start | bytes 9608 | tf_op jit(solution)/shard_map/ppermute | solution.py:562
  32.1 6.8 %collective-permute-start.10 = (f32[18,16,128]{2,1,0:T(8,128)S(1)}, f32[18,16,128]{2,1,0:T(8,128)S(1)}, u32[]{:S(2)}, u32[]{:S(2)}) collective-permute-start(f32[18,16,128]{2,1,0:T(8,128)S(1)} %get-tuple-element.37.refs_0_), channel_id=1, source_target_pairs={{0,4},{4,0},{1,5},{5,1},{2,6},{6,2},{3,7},{7,3},{8,12},{12,8},{9,1... | collective-permute-start | bytes 442376 | tf_op jit(solution)/shard_map/ppermute | solution.py:554
  32.7 6.6 %collective-permute-start.15 = (f32[18,16,128]{2,1,0:T(8,128)S(1)}, f32[18,16,128]{2,1,0:T(8,128)S(1)}, u32[]{:S(2)}, u32[]{:S(2)}) collective-permute-start(f32[18,16,128]{2,1,0:T(8,128)S(1)} %get-tuple-element.38.refs_8_), channel_id=1, source_target_pairs={{0,2},{1,3},{2,0},{3,1},{4,6},{5,7},{6,4},{7,5},{8,10},{9,11},{10,... | collective-permute-start | bytes 442376 | tf_op jit(solution)/shard_map/ppermute | solution.py:554
  33.2 7.5 %collective-permute-start.17 = (f32[18,16,128]{2,1,0:T(8,128)S(1)}, f32[18,16,128]{2,1,0:T(8,128)S(1)}, u32[]{:S(2)}, u32[]{:S(2)}) collective-permute-start(f32[18,16,128]{2,1,0:T(8,128)S(1)} %get-tuple-element.38.refs_8_), channel_id=1, source_target_pairs={{0,4},{4,0},{1,5},{5,1},{2,6},{6,2},{3,7},{7,3},{8,12},{12,8},{9,1... | collective-permute-start | bytes 442376 | tf_op jit(solution)/shard_map/ppermute | solution.py:554
  35.1 6.4 %collective-permute-start.8 = (f32[18,16,128]{2,1,0:T(8,128)S(1)}, f32[18,16,128]{2,1,0:T(8,128)S(1)}, u32[]{:S(2)}, u32[]{:S(2)}) collective-permute-start(f32[18,16,128]{2,1,0:T(8,128)S(1)} %get-tuple-element.37.refs_0_), channel_id=1, source_target_pairs={{0,2},{1,3},{2,0},{3,1},{4,6},{5,7},{6,4},{7,5},{8,10},{9,11},{10,... | collective-permute-start | bytes 442376 | tf_op jit(solution)/shard_map/ppermute | solution.py:554
  36.3 5.2 %collective-permute-start.14 = (f32[18,16,128]{2,1,0:T(8,128)S(1)}, f32[18,16,128]{2,1,0:T(8,128)S(1)}, u32[]{:S(2)}, u32[]{:S(2)}) collective-permute-start(f32[18,16,128]{2,1,0:T(8,128)S(1)} %get-tuple-element.38.refs_8_), channel_id=1, source_target_pairs={{0,1},{1,0},{2,3},{3,2},{4,5},{5,4},{6,7},{7,6},{8,9},{9,8},{10,11... | collective-permute-start | bytes 442376 | tf_op jit(solution)/shard_map/ppermute | solution.py:554
  38.9 3.1 %collective-permute-start.7 = (f32[18,16,128]{2,1,0:T(8,128)S(1)}, f32[18,16,128]{2,1,0:T(8,128)S(1)}, u32[]{:S(2)}, u32[]{:S(2)}) collective-permute-start(f32[18,16,128]{2,1,0:T(8,128)S(1)} %get-tuple-element.37.refs_0_), channel_id=1, source_target_pairs={{0,1},{1,0},{2,3},{3,2},{4,5},{5,4},{6,7},{7,6},{8,9},{9,8},{10,11... | collective-permute-start | bytes 442376 | tf_op jit(solution)/shard_map/ppermute | solution.py:554
  39.4 5.8 %collective-permute-start.12 = (f32[18,16,128]{2,1,0:T(8,128)S(1)}, f32[18,16,128]{2,1,0:T(8,128)S(1)}, u32[]{:S(2)}, u32[]{:S(2)}) collective-permute-start(f32[18,16,128]{2,1,0:T(8,128)S(1)} %collective-permute-done.10.refs_4_), channel_id=1, source_target_pairs={{0,2},{1,3},{2,0},{3,1},{4,6},{5,7},{6,4},{7,5},{8,10},{9,11},{10,... | collective-permute-start | bytes 442376 | tf_op jit(solution)/shard_map/ppermute | solution.py:554
  40.6 5.1 %collective-permute-start.19 = (f32[18,16,128]{2,1,0:T(8,128)S(1)}, f32[18,16,128]{2,1,0:T(8,128)S(1)}, u32[]{:S(2)}, u32[]{:S(2)}) collective-permute-start(f32[18,16,128]{2,1,0:T(8,128)S(1)} %collective-permute-done.15.refs_10_), channel_id=1, source_target_pairs={{0,4},{4,0},{1,5},{5,1},{2,6},{6,2},{3,7},{7,3},{8,12},{12,8},{9,1... | collective-permute-start | bytes 442376 | tf_op jit(solution)/shard_map/ppermute | solution.py:554
  41.5 4.3 %collective-permute-start.11 = (f32[18,16,128]{2,1,0:T(8,128)S(1)}, f32[18,16,128]{2,1,0:T(8,128)S(1)}, u32[]{:S(2)}, u32[]{:S(2)}) collective-permute-start(f32[18,16,128]{2,1,0:T(8,128)S(1)} %collective-permute-done.10.refs_4_), channel_id=1, source_target_pairs={{0,1},{1,0},{2,3},{3,2},{4,5},{5,4},{6,7},{7,6},{8,9},{9,8},{10,11... | collective-permute-start | bytes 442376 | tf_op jit(solution)/shard_map/ppermute | solution.py:554
  41.5 4.8 %collective-permute-start.16 = (f32[18,16,128]{2,1,0:T(8,128)S(1)}, f32[18,16,128]{2,1,0:T(8,128)S(1)}, u32[]{:S(2)}, u32[]{:S(2)}) collective-permute-start(f32[18,16,128]{2,1,0:T(8,128)S(1)} %collective-permute-done.15.refs_10_), channel_id=1, source_target_pairs={{0,1},{1,0},{2,3},{3,2},{4,5},{5,4},{6,7},{7,6},{8,9},{9,8},{10,11... | collective-permute-start | bytes 442376 | tf_op jit(solution)/shard_map/ppermute | solution.py:554
  42.0 4.3 %collective-permute-start.18 = (f32[18,16,128]{2,1,0:T(8,128)S(1)}, f32[18,16,128]{2,1,0:T(8,128)S(1)}, u32[]{:S(2)}, u32[]{:S(2)}) collective-permute-start(f32[18,16,128]{2,1,0:T(8,128)S(1)} %collective-permute-done.17.refs_12_), channel_id=1, source_target_pairs={{0,1},{1,0},{2,3},{3,2},{4,5},{5,4},{6,7},{7,6},{8,9},{9,8},{10,11... | collective-permute-start | bytes 442376 | tf_op jit(solution)/shard_map/ppermute | solution.py:554
  45.2 1.4 %collective-permute-start.9 = (f32[18,16,128]{2,1,0:T(8,128)S(1)}, f32[18,16,128]{2,1,0:T(8,128)S(1)}, u32[]{:S(2)}, u32[]{:S(2)}) collective-permute-start(f32[18,16,128]{2,1,0:T(8,128)S(1)} %collective-permute-done.8.refs_2_), channel_id=1, source_target_pairs={{0,1},{1,0},{2,3},{3,2},{4,5},{5,4},{6,7},{7,6},{8,9},{9,8},{10,11... | collective-permute-start | bytes 442376 | tf_op jit(solution)/shard_map/ppermute | solution.py:554
  45.8 1.6 %collective-permute-start.20 = (f32[18,16,128]{2,1,0:T(8,128)S(1)}, f32[18,16,128]{2,1,0:T(8,128)S(1)}, u32[]{:S(2)}, u32[]{:S(2)}) collective-permute-start(f32[18,16,128]{2,1,0:T(8,128)S(1)} %collective-permute-done.19.refs_14_), channel_id=1, source_target_pairs={{0,1},{1,0},{2,3},{3,2},{4,5},{5,4},{6,7},{7,6},{8,9},{9,8},{10,11... | collective-permute-start | bytes 442376 | tf_op jit(solution)/shard_map/ppermute | solution.py:554
  86.8 1.5 %collective-permute-start.21 = (f32[160,256]{1,0:T(8,128)S(1)}, f32[160,256]{1,0:T(8,128)S(1)}, u32[]{:S(2)}, u32[]{:S(2)}) collective-permute-start(f32[160,256]{1,0:T(8,128)S(1)} %get-tuple-element.47), channel_id=1, source_target_pairs={{0,1},{1,0},{2,3},{3,2},{4,5},{5,4},{6,7},{7,6},{8,9},{9,8},{10,11... | collective-permute-start | bytes 491528 | tf_op jit(solution)/shard_map/ppermute | solution.py:554
  88.3 4.1 %collective-permute-start.22 = (f32[40,256]{1,0:T(8,128)S(1)}, f32[40,256]{1,0:T(8,128)S(1)}, u32[]{:S(2)}, u32[]{:S(2)}) collective-permute-start(f32[40,256]{1,0:T(8,128)S(1)} %get-tuple-element.55), channel_id=1, source_target_pairs={{0,2},{1,3},{2,0},{3,1},{4,6},{5,7},{6,4},{7,5},{8,10},{9,11},{10,... | collective-permute-start | bytes 122888 | tf_op jit(solution)/shard_map/ppermute | solution.py:562
  89.5 4.0 %collective-permute-start.23 = (f32[40,256]{1,0:T(8,128)S(1)}, f32[40,256]{1,0:T(8,128)S(1)}, u32[]{:S(2)}, u32[]{:S(2)}) collective-permute-start(f32[40,256]{1,0:T(8,128)S(1)} %get-tuple-element.57), channel_id=1, source_target_pairs={{0,4},{1,5},{2,6},{3,7},{4,0},{5,1},{6,2},{7,3},{8,12},{9,13},{10,... | collective-permute-start | bytes 122888 | tf_op jit(solution)/shard_map/ppermute | solution.py:562
  90.5 4.9 %collective-permute-start.24 = (f32[40,256]{1,0:T(8,128)S(1)}, f32[40,256]{1,0:T(8,128)S(1)}, u32[]{:S(2)}, u32[]{:S(2)}) collective-permute-start(f32[40,256]{1,0:T(8,128)S(1)} %get-tuple-element.56), channel_id=1, source_target_pairs={{0,6},{1,7},{2,4},{3,5},{4,2},{5,3},{6,0},{7,1},{8,14},{9,15},{10,... | collective-permute-start | bytes 122888 | tf_op jit(solution)/shard_map/ppermute | solution.py:562
  95.5 4.1 %collective-permute-start.25 = (f32[40,256]{1,0:T(8,128)S(1)}, f32[40,256]{1,0:T(8,128)S(1)}, u32[]{:S(2)}, u32[]{:S(2)}) collective-permute-start(f32[40,256]{1,0:T(8,128)S(1)} %add_add_fusion), channel_id=1, source_target_pairs={{0,8},{8,0},{16,24},{24,16},{1,9},{9,1},{17,25},{25,17},{2,10},{10... | collective-permute-start | bytes 122888 | tf_op jit(solution)/shard_map/ppermute | solution.py:554
  99.5 4.9 %collective-permute-start.26 = (f32[40,256]{1,0:T(8,128)S(1)}, f32[40,256]{1,0:T(8,128)S(1)}, u32[]{:S(2)}, u32[]{:S(2)}) collective-permute-start(f32[40,256]{1,0:T(8,128)S(1)} %add.58), channel_id=1, source_target_pairs={{0,16},{8,24},{16,0},{24,8},{1,17},{9,25},{17,1},{25,9},{2,18},{10... | collective-permute-start | bytes 122888 | tf_op jit(solution)/shard_map/ppermute | solution.py:554
  104.4 4.0 %collective-permute-start.27 = (f32[40,256]{1,0:T(8,128)S(1)}, f32[40,256]{1,0:T(8,128)S(1)}, u32[]{:S(2)}, u32[]{:S(2)}) collective-permute-start(f32[40,256]{1,0:T(8,128)S(1)} %add.59.refs_0_), channel_id=1, source_target_pairs={{0,2},{1,3},{2,0},{3,1},{4,6},{5,7},{6,4},{7,5},{8,10},{9,11},{10,... | collective-permute-start | bytes 122888 | tf_op jit(solution)/shard_map/ppermute | solution.py:562
  105.1 4.0 %collective-permute-start.28 = (f32[40,256]{1,0:T(8,128)S(1)}, f32[40,256]{1,0:T(8,128)S(1)}, u32[]{:S(2)}, u32[]{:S(2)}) collective-permute-start(f32[40,256]{1,0:T(8,128)S(1)} %add.59.refs_0_), channel_id=1, source_target_pairs={{0,4},{1,5},{2,6},{3,7},{4,0},{5,1},{6,2},{7,3},{8,12},{9,13},{10,... | collective-permute-start | bytes 122888 | tf_op jit(solution)/shard_map/ppermute | solution.py:562
  106.3 4.9 %collective-permute-start.29 = (f32[40,256]{1,0:T(8,128)S(1)}, f32[40,256]{1,0:T(8,128)S(1)}, u32[]{:S(2)}, u32[]{:S(2)}) collective-permute-start(f32[40,256]{1,0:T(8,128)S(1)} %add.59.refs_0_), channel_id=1, source_target_pairs={{0,6},{1,7},{2,4},{3,5},{4,2},{5,3},{6,0},{7,1},{8,14},{9,15},{10,... | collective-permute-start | bytes 122888 | tf_op jit(solution)/shard_map/ppermute | solution.py:562
  107.9 3.3 %collective-permute-start.30 = (f32[40,256]{1,0:T(8,128)S(1)}, f32[40,256]{1,0:T(8,128)S(1)}, u32[]{:S(2)}, u32[]{:S(2)}) collective-permute-start(f32[40,256]{1,0:T(8,128)S(1)} %add.59.refs_0_), channel_id=1, source_target_pairs={{0,1},{1,0},{2,3},{3,2},{4,5},{5,4},{6,7},{7,6},{8,9},{9,8},{10,11... | collective-permute-start | bytes 122888 | tf_op jit(solution)/shard_map/ppermute | solution.py:554
  108.4 2.8 %collective-permute-start.31 = (f32[40,256]{1,0:T(8,128)S(1)}, f32[40,256]{1,0:T(8,128)S(1)}, u32[]{:S(2)}, u32[]{:S(2)}) collective-permute-start(f32[40,256]{1,0:T(8,128)S(1)} %collective-permute-done.27.refs_1_), channel_id=1, source_target_pairs={{0,1},{1,0},{2,3},{3,2},{4,5},{5,4},{6,7},{7,6},{8,9},{9,8},{10,11... | collective-permute-start | bytes 122888 | tf_op jit(solution)/shard_map/ppermute | solution.py:554
  109.1 2.1 %collective-permute-start.32 = (f32[40,256]{1,0:T(8,128)S(1)}, f32[40,256]{1,0:T(8,128)S(1)}, u32[]{:S(2)}, u32[]{:S(2)}) collective-permute-start(f32[40,256]{1,0:T(8,128)S(1)} %collective-permute-done.28.refs_2_), channel_id=1, source_target_pairs={{0,1},{1,0},{2,3},{3,2},{4,5},{5,4},{6,7},{7,6},{8,9},{9,8},{10,11... | collective-permute-start | bytes 122888 | tf_op jit(solution)/shard_map/ppermute | solution.py:554
  (2 other events, 2.6 us)
